TPU v7x, 128 devices: a whole 4x4x4 slice. The times are simulated.
128 devices in a mesh: tm: 4 (over x_lo, core), space: 32 (over x_hi, y, z).
Axes of the slice: x: 4 (x_hi: 2, x_lo: 2; x = x_hi * 2 + x_lo), y: 4, z: 4, core: 2. Of those that a mesh axis runs over, the one named last changes fastest.
Arguments:
- forcing: bfloat16 [4, 4, 6, 256, 4096], P('tm', None, None, None, 'space'), may hold values from -6 to 6
- zonal_courant: float32 [4, 256, 4096], P('tm', None, 'space'), may hold values from -0.3 to 0.3
- meridional_courant: float32 [4, 256, 4096], P('tm', None, 'space'), may hold values from -0.3 to 0.3
- zonal_faces: float32 [4, 256, 4096], P('tm', None, 'space'), may hold values from 0.1 to 0.4
- meridional_faces: float32 [4, 256, 4096], P('tm', None, 'space'), may hold values from 0.1 to 0.4
- coupling: float32 [4, 6, 6], P('tm'), may hold values from -0.375 to 0.375
Outputs:
- adjoint_start: float32 [4, 6, 256, 4096], P('tm', None, None, 'space')
All inputs are finite; a program needn't handle non-finite values.
Results may differ from a plain program's by a relative error of at most 0.0015.
Values may be sent and summed in bfloat16 or wider, within the bound.
A program may use at most 64 MiB of HBM per device.

v0:
```python
import jax
import jax.numpy as jnp
from jax import lax
from jax.sharding import PartitionSpec as P

STEPS = 4
SWEEPS = 2


OMEGA = 0.4


def with_halo(shard, sides, width):
    for axis, dim in sides:
        count, length = (lax.axis_size(axis), shard.shape[dim])
        up = [(i, (i + 1) % count) for i in range(count)]
        down = [(j, i) for i, j in up]
        last = lax.slice_in_dim(shard, length - width, length, axis=dim)
        leading = lax.slice_in_dim(shard, 0, width, axis=dim)
        before = lax.ppermute(last, axis, up)
        after = lax.ppermute(leading, axis, down)
        shard = jnp.concatenate([before, shard, after], axis=dim)
    return shard


def shifted(block, axis, distance):
    devices = range(lax.axis_size(axis))
    route = [((i - distance) % len(devices), i) for i in devices]
    return lax.ppermute(block, axis, route)


def shifted_2(shard, axis, by):
    count = lax.axis_size(axis)
    pairs = [(i, i + by) for i in range(count) if 0 <= i + by < count]
    return lax.ppermute(shard, axis, pairs)


def north(values):
    zero_edge = jnp.zeros_like(values[..., :1, :])
    return jnp.concatenate([values[..., 1:, :], zero_edge], axis=-2)


def south(values):
    zero_edge = jnp.zeros_like(values[..., :1, :])
    return jnp.concatenate([zero_edge, values[..., :-1, :]], axis=-2)


def east_local(values):
    zero_edge = jnp.zeros_like(values[..., :1])
    return jnp.concatenate([values[..., 1:], zero_edge], axis=-1)


def west_local(values):
    zero_edge = jnp.zeros_like(values[..., :1])
    return jnp.concatenate([zero_edge, values[..., :-1]], axis=-1)


def apply_operator(state_now, east_side, west_side, face_set):
    face_east, face_west, face_north, face_south = face_set
    return (
        state_now
        + face_east * (state_now - east_side)
        + face_west * (state_now - west_side)
        + face_north * (state_now - north(state_now))
        + face_south * (state_now - south(state_now))
    )


def mix_and_meridional(smoothed, courant_y, coupling_now):
    meridional_flux = courant_y * smoothed
    mixing = jnp.einsum("gf,gab->fab", coupling_now, smoothed, precision=lax.Precision.HIGHEST)
    return smoothed + mixing + 0.5 * (north(meridional_flux) - south(meridional_flux))


def strip_step(adjoint, forcing_step, courant_x, courant_y, face_set, coupling_now):
    smoothed = OMEGA * adjoint
    for sweep_index in range(SWEEPS):
        padded = with_halo(smoothed.astype(jnp.bfloat16), (("space", 2),), 1).astype(smoothed.dtype)
        smoothed = smoothed + OMEGA * (
            adjoint - apply_operator(smoothed, padded[..., 2:], padded[..., :-2], face_set)
        )
    flux_term = courant_x * smoothed
    zonal_term = 0.5 * (east_local(flux_term) - west_local(flux_term))
    rim_terms = jnp.stack([0.5 * flux_term[..., 0], -0.5 * flux_term[..., -1]], axis=0)
    arrived = with_halo(rim_terms, (("space", 0),), 1)
    zonal_term = zonal_term.at[..., 0].add(arrived[0]).at[..., -1].add(arrived[3])
    return (
        mix_and_meridional(smoothed, courant_y, coupling_now)
        + zonal_term
        + forcing_step.astype(jnp.float32)
    )


def per_device(forcing, zonal_courant, meridional_courant, zonal_faces, meridional_faces, coupling):
    row_index = lax.broadcasted_iota(jnp.int32, meridional_faces.shape, 1)
    northern = jnp.where(
        row_index < meridional_faces.shape[1] - 1,
        meridional_faces,
        jnp.zeros_like(meridional_faces),
    )
    western = shifted(zonal_faces[..., -1], "space", 1)
    start_state = jnp.zeros(forcing.shape[2:], jnp.float32)
    incoming = start_state
    rounds_total = lax.axis_size("tm")
    result = start_state
    for round_index in range(rounds_total):
        adjoint = incoming
        face_west = jnp.concatenate([western[0][:, None], zonal_faces[0][:, :-1]], axis=-1)
        face_set = (zonal_faces[0], face_west, northern[0], south(northern[0]))
        for step_index in reversed(range(STEPS)):
            adjoint = strip_step(
                adjoint,
                forcing[0, step_index],
                zonal_courant[0],
                meridional_courant[0],
                face_set,
                coupling[0],
            )
        result = adjoint
        if round_index + 1 < rounds_total:
            incoming = shifted_2(result.astype(jnp.bfloat16), "tm", -1).astype(result.dtype)
    return result[None]


def solution(mesh):
    return jax.shard_map(
        per_device,
        mesh=mesh,
        in_specs=(
            P("tm", None, None, None, "space"),
            P("tm", None, "space"),
            P("tm", None, "space"),
            P("tm", None, "space"),
            P("tm", None, "space"),
            P("tm", None, None),
        ),
        out_specs=P("tm", None, None, "space"),
        check_vma=False,
    )
```

profile of v0, /device:TPU:2, one launch (start us, length us, event | category | flops | bytes accessed | tf_op | source)
XLA Modules:
  0.0 679.9 jit_solution(18005230554179616274)
XLA Ops:
  0.0 8.1 %collective-permute-start.1 = (bf16[6,256,1]{1,0,2:T(8,128)(2,1)S(1)}, bf16[6,256,1]{1,0,2:T(8,128)(2,1)S(1)}, u32[]{:S(2)}, u32[]{:S(2)}) collective-permute-start(bf16[6,256,1]{1,0,2:T(8,128)(2,1)S(1)} %slice.1602), channel_id=1, source_target_pairs={{1,0},{2,1},{3,2},{4,3},{5,4},{6,5},{7,6},{8,7},{9,8},{10,9},{11,1... | collective-permute-start | bytes 9224 | tf_op jit(solution)/shard_map/ppermute | solution.py:21
  21.2 7.7 %collective-permute-start.4 = (bf16[6,256,1]{1,0,2:T(8,128)(2,1)S(1)}, bf16[6,256,1]{1,0,2:T(8,128)(2,1)S(1)}, u32[]{:S(2)}, u32[]{:S(2)}) collective-permute-start(bf16[6,256,1]{1,0,2:T(8,128)(2,1)S(1)} %get-tuple-element.706), channel_id=1, source_target_pairs={{1,0},{2,1},{3,2},{4,3},{5,4},{6,5},{7,6},{8,7},{9,8},{10,9},{11,1... | collective-permute-start | bytes 9224 | tf_op jit(solution)/shard_map/ppermute | solution.py:21
  31.7 7.8 %collective-permute-start.6 = (f32[1,6,256]{2,1,0:T(8,128)S(1)}, f32[1,6,256]{2,1,0:T(8,128)S(1)}, u32[]{:S(2)}, u32[]{:S(2)}) collective-permute-start(f32[1,6,256]{2,1,0:T(8,128)S(1)} %get-tuple-element.633), channel_id=1, source_target_pairs={{1,0},{2,1},{3,2},{4,3},{5,4},{6,5},{7,6},{8,7},{9,8},{10,9},{11,1... | collective-permute-start | bytes 18440 | tf_op jit(solution)/shard_map/ppermute | solution.py:21
  40.1 8.9 %collective-permute-done.5 = f32[1,6,256]{2,1,0:T(8,128)S(1)} collective-permute-done((f32[1,6,256]{2,1,0:T(8,128)S(1)}, f32[1,6,256]{2,1,0:T(8,128)S(1)}, u32[]{:S(2)}, u32[]{:S(2)}) %collective-permute-start.5) | collective-permute-done | bytes 6176 | tf_op jit(solution)/shard_map/ppermute | solution.py:20
  50.6 7.7 %collective-permute-start.8 = (bf16[6,256,1]{1,0,2:T(8,128)(2,1)S(1)}, bf16[6,256,1]{1,0,2:T(8,128)(2,1)S(1)}, u32[]{:S(2)}, u32[]{:S(2)}) collective-permute-start(bf16[6,256,1]{1,0,2:T(8,128)(2,1)S(1)} %get-tuple-element.704), channel_id=1, source_target_pairs={{1,0},{2,1},{3,2},{4,3},{5,4},{6,5},{7,6},{8,7},{9,8},{10,9},{11,1... | collective-permute-start | bytes 9224 | tf_op jit(solution)/shard_map/ppermute | solution.py:21
  61.0 8.3 %collective-permute-start.10 = (bf16[6,256,1]{1,0,2:T(8,128)(2,1)S(1)}, bf16[6,256,1]{1,0,2:T(8,128)(2,1)S(1)}, u32[]{:S(2)}, u32[]{:S(2)}) collective-permute-start(bf16[6,256,1]{1,0,2:T(8,128)(2,1)S(1)} %get-tuple-element.702), channel_id=1, source_target_pairs={{1,0},{2,1},{3,2},{4,3},{5,4},{6,5},{7,6},{8,7},{9,8},{10,9},{11,1... | collective-permute-start | bytes 9224 | tf_op jit(solution)/shard_map/ppermute | solution.py:21
  71.9 8.1 %collective-permute-start.12 = (f32[1,6,256]{2,1,0:T(8,128)S(1)}, f32[1,6,256]{2,1,0:T(8,128)S(1)}, u32[]{:S(2)}, u32[]{:S(2)}) collective-permute-start(f32[1,6,256]{2,1,0:T(8,128)S(1)} %get-tuple-element.621), channel_id=1, source_target_pairs={{1,0},{2,1},{3,2},{4,3},{5,4},{6,5},{7,6},{8,7},{9,8},{10,9},{11,1... | collective-permute-start | bytes 18440 | tf_op jit(solution)/shard_map/ppermute | solution.py:21
  80.5 8.9 %collective-permute-done.11 = f32[1,6,256]{2,1,0:T(8,128)S(1)} collective-permute-done((f32[1,6,256]{2,1,0:T(8,128)S(1)}, f32[1,6,256]{2,1,0:T(8,128)S(1)}, u32[]{:S(2)}, u32[]{:S(2)}) %collective-permute-start.11) | collective-permute-done | bytes 6176 | tf_op jit(solution)/shard_map/ppermute | solution.py:20
  91.1 7.7 %collective-permute-start.14 = (bf16[6,256,1]{1,0,2:T(8,128)(2,1)S(1)}, bf16[6,256,1]{1,0,2:T(8,128)(2,1)S(1)}, u32[]{:S(2)}, u32[]{:S(2)}) collective-permute-start(bf16[6,256,1]{1,0,2:T(8,128)(2,1)S(1)} %get-tuple-element.700), channel_id=1, source_target_pairs={{1,0},{2,1},{3,2},{4,3},{5,4},{6,5},{7,6},{8,7},{9,8},{10,9},{11,1... | collective-permute-start | bytes 9224 | tf_op jit(solution)/shard_map/ppermute | solution.py:21
  101.4 7.8 %collective-permute-start.16 = (bf16[6,256,1]{1,0,2:T(8,128)(2,1)S(1)}, bf16[6,256,1]{1,0,2:T(8,128)(2,1)S(1)}, u32[]{:S(2)}, u32[]{:S(2)}) collective-permute-start(bf16[6,256,1]{1,0,2:T(8,128)(2,1)S(1)} %get-tuple-element.698), channel_id=1, source_target_pairs={{1,0},{2,1},{3,2},{4,3},{5,4},{6,5},{7,6},{8,7},{9,8},{10,9},{11,1... | collective-permute-start | bytes 9224 | tf_op jit(solution)/shard_map/ppermute | solution.py:21
  112.0 7.9 %collective-permute-start.18 = (f32[1,6,256]{2,1,0:T(8,128)S(1)}, f32[1,6,256]{2,1,0:T(8,128)S(1)}, u32[]{:S(2)}, u32[]{:S(2)}) collective-permute-start(f32[1,6,256]{2,1,0:T(8,128)S(1)} %get-tuple-element.609), channel_id=1, source_target_pairs={{1,0},{2,1},{3,2},{4,3},{5,4},{6,5},{7,6},{8,7},{9,8},{10,9},{11,1... | collective-permute-start | bytes 18440 | tf_op jit(solution)/shard_map/ppermute | solution.py:21
  120.4 8.9 %collective-permute-done.17 = f32[1,6,256]{2,1,0:T(8,128)S(1)} collective-permute-done((f32[1,6,256]{2,1,0:T(8,128)S(1)}, f32[1,6,256]{2,1,0:T(8,128)S(1)}, u32[]{:S(2)}, u32[]{:S(2)}) %collective-permute-start.17) | collective-permute-done | bytes 6176 | tf_op jit(solution)/shard_map/ppermute | solution.py:20
  131.0 7.9 %collective-permute-start.20 = (bf16[6,256,1]{1,0,2:T(8,128)(2,1)S(1)}, bf16[6,256,1]{1,0,2:T(8,128)(2,1)S(1)}, u32[]{:S(2)}, u32[]{:S(2)}) collective-permute-start(bf16[6,256,1]{1,0,2:T(8,128)(2,1)S(1)} %get-tuple-element.696), channel_id=1, source_target_pairs={{1,0},{2,1},{3,2},{4,3},{5,4},{6,5},{7,6},{8,7},{9,8},{10,9},{11,1... | collective-permute-start | bytes 9224 | tf_op jit(solution)/shard_map/ppermute | solution.py:21
  141.4 8.0 %collective-permute-start.22 = (bf16[6,256,1]{1,0,2:T(8,128)(2,1)S(1)}, bf16[6,256,1]{1,0,2:T(8,128)(2,1)S(1)}, u32[]{:S(2)}, u32[]{:S(2)}) collective-permute-start(bf16[6,256,1]{1,0,2:T(8,128)(2,1)S(1)} %get-tuple-element.694), channel_id=1, source_target_pairs={{1,0},{2,1},{3,2},{4,3},{5,4},{6,5},{7,6},{8,7},{9,8},{10,9},{11,1... | collective-permute-start | bytes 9224 | tf_op jit(solution)/shard_map/ppermute | solution.py:21
  152.2 7.9 %collective-permute-start.24 = (f32[1,6,256]{2,1,0:T(8,128)S(1)}, f32[1,6,256]{2,1,0:T(8,128)S(1)}, u32[]{:S(2)}, u32[]{:S(2)}) collective-permute-start(f32[1,6,256]{2,1,0:T(8,128)S(1)} %get-tuple-element.597), channel_id=1, source_target_pairs={{1,0},{2,1},{3,2},{4,3},{5,4},{6,5},{7,6},{8,7},{9,8},{10,9},{11,1... | collective-permute-start | bytes 18440 | tf_op jit(solution)/shard_map/ppermute | solution.py:21
  160.6 8.9 %collective-permute-done.23 = f32[1,6,256]{2,1,0:T(8,128)S(1)} collective-permute-done((f32[1,6,256]{2,1,0:T(8,128)S(1)}, f32[1,6,256]{2,1,0:T(8,128)S(1)}, u32[]{:S(2)}, u32[]{:S(2)}) %collective-permute-start.23) | collective-permute-done | bytes 6176 | tf_op jit(solution)/shard_map/ppermute | solution.py:20
  179.9 7.7 %collective-permute-start.27 = (bf16[6,256,1]{1,0,2:T(8,128)(2,1)S(1)}, bf16[6,256,1]{1,0,2:T(8,128)(2,1)S(1)}, u32[]{:S(2)}, u32[]{:S(2)}) collective-permute-start(bf16[6,256,1]{1,0,2:T(8,128)(2,1)S(1)} %get-tuple-element.690), channel_id=1, source_target_pairs={{1,0},{2,1},{3,2},{4,3},{5,4},{6,5},{7,6},{8,7},{9,8},{10,9},{11,1... | collective-permute-start | bytes 9224 | tf_op jit(solution)/shard_map/ppermute | solution.py:21
  190.2 7.8 %collective-permute-start.29 = (bf16[6,256,1]{1,0,2:T(8,128)(2,1)S(1)}, bf16[6,256,1]{1,0,2:T(8,128)(2,1)S(1)}, u32[]{:S(2)}, u32[]{:S(2)}) collective-permute-start(bf16[6,256,1]{1,0,2:T(8,128)(2,1)S(1)} %get-tuple-element.688), channel_id=1, source_target_pairs={{1,0},{2,1},{3,2},{4,3},{5,4},{6,5},{7,6},{8,7},{9,8},{10,9},{11,1... | collective-permute-start | bytes 9224 | tf_op jit(solution)/shard_map/ppermute | solution.py:21
  200.9 7.9 %collective-permute-start.31 = (f32[1,6,256]{2,1,0:T(8,128)S(1)}, f32[1,6,256]{2,1,0:T(8,128)S(1)}, u32[]{:S(2)}, u32[]{:S(2)}) collective-permute-start(f32[1,6,256]{2,1,0:T(8,128)S(1)} %get-tuple-element.587), channel_id=1, source_target_pairs={{1,0},{2,1},{3,2},{4,3},{5,4},{6,5},{7,6},{8,7},{9,8},{10,9},{11,1... | collective-permute-start | bytes 18440 | tf_op jit(solution)/shard_map/ppermute | solution.py:21
  209.5 8.9 %collective-permute-done.30 = f32[1,6,256]{2,1,0:T(8,128)S(1)} collective-permute-done((f32[1,6,256]{2,1,0:T(8,128)S(1)}, f32[1,6,256]{2,1,0:T(8,128)S(1)}, u32[]{:S(2)}, u32[]{:S(2)}) %collective-permute-start.30) | collective-permute-done | bytes 6176 | tf_op jit(solution)/shard_map/ppermute | solution.py:20
  220.0 7.7 %collective-permute-start.33 = (bf16[6,256,1]{1,0,2:T(8,128)(2,1)S(1)}, bf16[6,256,1]{1,0,2:T(8,128)(2,1)S(1)}, u32[]{:S(2)}, u32[]{:S(2)}) collective-permute-start(bf16[6,256,1]{1,0,2:T(8,128)(2,1)S(1)} %get-tuple-element.686), channel_id=1, source_target_pairs={{1,0},{2,1},{3,2},{4,3},{5,4},{6,5},{7,6},{8,7},{9,8},{10,9},{11,1... | collective-permute-start | bytes 9224 | tf_op jit(solution)/shard_map/ppermute | solution.py:21
  230.4 7.8 %collective-permute-start.35 = (bf16[6,256,1]{1,0,2:T(8,128)(2,1)S(1)}, bf16[6,256,1]{1,0,2:T(8,128)(2,1)S(1)}, u32[]{:S(2)}, u32[]{:S(2)}) collective-permute-start(bf16[6,256,1]{1,0,2:T(8,128)(2,1)S(1)} %get-tuple-element.684), channel_id=1, source_target_pairs={{1,0},{2,1},{3,2},{4,3},{5,4},{6,5},{7,6},{8,7},{9,8},{10,9},{11,1... | collective-permute-start | bytes 9224 | tf_op jit(solution)/shard_map/ppermute | solution.py:21
  241.0 7.9 %collective-permute-start.37 = (f32[1,6,256]{2,1,0:T(8,128)S(1)}, f32[1,6,256]{2,1,0:T(8,128)S(1)}, u32[]{:S(2)}, u32[]{:S(2)}) collective-permute-start(f32[1,6,256]{2,1,0:T(8,128)S(1)} %get-tuple-element.575), channel_id=1, source_target_pairs={{1,0},{2,1},{3,2},{4,3},{5,4},{6,5},{7,6},{8,7},{9,8},{10,9},{11,1... | collective-permute-start | bytes 18440 | tf_op jit(solution)/shard_map/ppermute | solution.py:21
  249.4 8.9 %collective-permute-done.36 = f32[1,6,256]{2,1,0:T(8,128)S(1)} collective-permute-done((f32[1,6,256]{2,1,0:T(8,128)S(1)}, f32[1,6,256]{2,1,0:T(8,128)S(1)}, u32[]{:S(2)}, u32[]{:S(2)}) %collective-permute-start.36) | collective-permute-done | bytes 6176 | tf_op jit(solution)/shard_map/ppermute | solution.py:20
  260.0 7.7 %collective-permute-start.39 = (bf16[6,256,1]{1,0,2:T(8,128)(2,1)S(1)}, bf16[6,256,1]{1,0,2:T(8,128)(2,1)S(1)}, u32[]{:S(2)}, u32[]{:S(2)}) collective-permute-start(bf16[6,256,1]{1,0,2:T(8,128)(2,1)S(1)} %get-tuple-element.682), channel_id=1, source_target_pairs={{1,0},{2,1},{3,2},{4,3},{5,4},{6,5},{7,6},{8,7},{9,8},{10,9},{11,1... | collective-permute-start | bytes 9224 | tf_op jit(solution)/shard_map/ppermute | solution.py:21
  270.3 8.2 %collective-permute-start.41 = (bf16[6,256,1]{1,0,2:T(8,128)(2,1)S(1)}, bf16[6,256,1]{1,0,2:T(8,128)(2,1)S(1)}, u32[]{:S(2)}, u32[]{:S(2)}) collective-permute-start(bf16[6,256,1]{1,0,2:T(8,128)(2,1)S(1)} %get-tuple-element.680), channel_id=1, source_target_pairs={{1,0},{2,1},{3,2},{4,3},{5,4},{6,5},{7,6},{8,7},{9,8},{10,9},{11,1... | collective-permute-start | bytes 9224 | tf_op jit(solution)/shard_map/ppermute | solution.py:21
  281.2 8.1 %collective-permute-start.43 = (f32[1,6,256]{2,1,0:T(8,128)S(1)}, f32[1,6,256]{2,1,0:T(8,128)S(1)}, u32[]{:S(2)}, u32[]{:S(2)}) collective-permute-start(f32[1,6,256]{2,1,0:T(8,128)S(1)} %get-tuple-element.563), channel_id=1, source_target_pairs={{1,0},{2,1},{3,2},{4,3},{5,4},{6,5},{7,6},{8,7},{9,8},{10,9},{11,1... | collective-permute-start | bytes 18440 | tf_op jit(solution)/shard_map/ppermute | solution.py:21
  289.8 8.9 %collective-permute-done.42 = f32[1,6,256]{2,1,0:T(8,128)S(1)} collective-permute-done((f32[1,6,256]{2,1,0:T(8,128)S(1)}, f32[1,6,256]{2,1,0:T(8,128)S(1)}, u32[]{:S(2)}, u32[]{:S(2)}) %collective-permute-start.42) | collective-permute-done | bytes 6176 | tf_op jit(solution)/shard_map/ppermute | solution.py:20
  300.3 7.7 %collective-permute-start.45 = (bf16[6,256,1]{1,0,2:T(8,128)(2,1)S(1)}, bf16[6,256,1]{1,0,2:T(8,128)(2,1)S(1)}, u32[]{:S(2)}, u32[]{:S(2)}) collective-permute-start(bf16[6,256,1]{1,0,2:T(8,128)(2,1)S(1)} %get-tuple-element.678), channel_id=1, source_target_pairs={{1,0},{2,1},{3,2},{4,3},{5,4},{6,5},{7,6},{8,7},{9,8},{10,9},{11,1... | collective-permute-start | bytes 9224 | tf_op jit(solution)/shard_map/ppermute | solution.py:21
  310.7 7.8 %collective-permute-start.47 = (bf16[6,256,1]{1,0,2:T(8,128)(2,1)S(1)}, bf16[6,256,1]{1,0,2:T(8,128)(2,1)S(1)}, u32[]{:S(2)}, u32[]{:S(2)}) collective-permute-start(bf16[6,256,1]{1,0,2:T(8,128)(2,1)S(1)} %get-tuple-element.676), channel_id=1, source_target_pairs={{1,0},{2,1},{3,2},{4,3},{5,4},{6,5},{7,6},{8,7},{9,8},{10,9},{11,1... | collective-permute-start | bytes 9224 | tf_op jit(solution)/shard_map/ppermute | solution.py:21
  321.3 7.9 %collective-permute-start.49 = (f32[1,6,256]{2,1,0:T(8,128)S(1)}, f32[1,6,256]{2,1,0:T(8,128)S(1)}, u32[]{:S(2)}, u32[]{:S(2)}) collective-permute-start(f32[1,6,256]{2,1,0:T(8,128)S(1)} %get-tuple-element.551), channel_id=1, source_target_pairs={{1,0},{2,1},{3,2},{4,3},{5,4},{6,5},{7,6},{8,7},{9,8},{10,9},{11,1... | collective-permute-start | bytes 18440 | tf_op jit(solution)/shard_map/ppermute | solution.py:21
  329.7 8.9 %collective-permute-done.48 = f32[1,6,256]{2,1,0:T(8,128)S(1)} collective-permute-done((f32[1,6,256]{2,1,0:T(8,128)S(1)}, f32[1,6,256]{2,1,0:T(8,128)S(1)}, u32[]{:S(2)}, u32[]{:S(2)}) %collective-permute-start.48) | collective-permute-done | bytes 6176 | tf_op jit(solution)/shard_map/ppermute | solution.py:20
  349.0 7.9 %collective-permute-start.52 = (bf16[6,256,1]{1,0,2:T(8,128)(2,1)S(1)}, bf16[6,256,1]{1,0,2:T(8,128)(2,1)S(1)}, u32[]{:S(2)}, u32[]{:S(2)}) collective-permute-start(bf16[6,256,1]{1,0,2:T(8,128)(2,1)S(1)} %get-tuple-element.672), channel_id=1, source_target_pairs={{1,0},{2,1},{3,2},{4,3},{5,4},{6,5},{7,6},{8,7},{9,8},{10,9},{11,1... | collective-permute-start | bytes 9224 | tf_op jit(solution)/shard_map/ppermute | solution.py:21
  359.4 8.0 %collective-permute-start.54 = (bf16[6,256,1]{1,0,2:T(8,128)(2,1)S(1)}, bf16[6,256,1]{1,0,2:T(8,128)(2,1)S(1)}, u32[]{:S(2)}, u32[]{:S(2)}) collective-permute-start(bf16[6,256,1]{1,0,2:T(8,128)(2,1)S(1)} %get-tuple-element.670), channel_id=1, source_target_pairs={{1,0},{2,1},{3,2},{4,3},{5,4},{6,5},{7,6},{8,7},{9,8},{10,9},{11,1... | collective-permute-start | bytes 9224 | tf_op jit(solution)/shard_map/ppermute | solution.py:21
  370.2 7.9 %collective-permute-start.56 = (f32[1,6,256]{2,1,0:T(8,128)S(1)}, f32[1,6,256]{2,1,0:T(8,128)S(1)}, u32[]{:S(2)}, u32[]{:S(2)}) collective-permute-start(f32[1,6,256]{2,1,0:T(8,128)S(1)} %get-tuple-element.541), channel_id=1, source_target_pairs={{1,0},{2,1},{3,2},{4,3},{5,4},{6,5},{7,6},{8,7},{9,8},{10,9},{11,1... | collective-permute-start | bytes 18440 | tf_op jit(solution)/shard_map/ppermute | solution.py:21
  378.6 8.9 %collective-permute-done.55 = f32[1,6,256]{2,1,0:T(8,128)S(1)} collective-permute-done((f32[1,6,256]{2,1,0:T(8,128)S(1)}, f32[1,6,256]{2,1,0:T(8,128)S(1)}, u32[]{:S(2)}, u32[]{:S(2)}) %collective-permute-start.55) | collective-permute-done | bytes 6176 | tf_op jit(solution)/shard_map/ppermute | solution.py:20
  389.2 7.7 %collective-permute-start.58 = (bf16[6,256,1]{1,0,2:T(8,128)(2,1)S(1)}, bf16[6,256,1]{1,0,2:T(8,128)(2,1)S(1)}, u32[]{:S(2)}, u32[]{:S(2)}) collective-permute-start(bf16[6,256,1]{1,0,2:T(8,128)(2,1)S(1)} %get-tuple-element.668), channel_id=1, source_target_pairs={{1,0},{2,1},{3,2},{4,3},{5,4},{6,5},{7,6},{8,7},{9,8},{10,9},{11,1... | collective-permute-start | bytes 9224 | tf_op jit(solution)/shard_map/ppermute | solution.py:21
  399.5 7.8 %collective-permute-start.60 = (bf16[6,256,1]{1,0,2:T(8,128)(2,1)S(1)}, bf16[6,256,1]{1,0,2:T(8,128)(2,1)S(1)}, u32[]{:S(2)}, u32[]{:S(2)}) collective-permute-start(bf16[6,256,1]{1,0,2:T(8,128)(2,1)S(1)} %get-tuple-element.666), channel_id=1, source_target_pairs={{1,0},{2,1},{3,2},{4,3},{5,4},{6,5},{7,6},{8,7},{9,8},{10,9},{11,1... | collective-permute-start | bytes 9224 | tf_op jit(solution)/shard_map/ppermute | solution.py:21
  410.2 7.9 %collective-permute-start.62 = (f32[1,6,256]{2,1,0:T(8,128)S(1)}, f32[1,6,256]{2,1,0:T(8,128)S(1)}, u32[]{:S(2)}, u32[]{:S(2)}) collective-permute-start(f32[1,6,256]{2,1,0:T(8,128)S(1)} %get-tuple-element.529), channel_id=1, source_target_pairs={{1,0},{2,1},{3,2},{4,3},{5,4},{6,5},{7,6},{8,7},{9,8},{10,9},{11,1... | collective-permute-start | bytes 18440 | tf_op jit(solution)/shard_map/ppermute | solution.py:21
  418.8 8.9 %collective-permute-done.61 = f32[1,6,256]{2,1,0:T(8,128)S(1)} collective-permute-done((f32[1,6,256]{2,1,0:T(8,128)S(1)}, f32[1,6,256]{2,1,0:T(8,128)S(1)}, u32[]{:S(2)}, u32[]{:S(2)}) %collective-permute-start.61) | collective-permute-done | bytes 6176 | tf_op jit(solution)/shard_map/ppermute | solution.py:20
  429.3 7.7 %collective-permute-start.64 = (bf16[6,256,1]{1,0,2:T(8,128)(2,1)S(1)}, bf16[6,256,1]{1,0,2:T(8,128)(2,1)S(1)}, u32[]{:S(2)}, u32[]{:S(2)}) collective-permute-start(bf16[6,256,1]{1,0,2:T(8,128)(2,1)S(1)} %get-tuple-element.664), channel_id=1, source_target_pairs={{1,0},{2,1},{3,2},{4,3},{5,4},{6,5},{7,6},{8,7},{9,8},{10,9},{11,1... | collective-permute-start | bytes 9224 | tf_op jit(solution)/shard_map/ppermute | solution.py:21
  439.7 7.8 %collective-permute-start.66 = (bf16[6,256,1]{1,0,2:T(8,128)(2,1)S(1)}, bf16[6,256,1]{1,0,2:T(8,128)(2,1)S(1)}, u32[]{:S(2)}, u32[]{:S(2)}) collective-permute-start(bf16[6,256,1]{1,0,2:T(8,128)(2,1)S(1)} %get-tuple-element.662), channel_id=1, source_target_pairs={{1,0},{2,1},{3,2},{4,3},{5,4},{6,5},{7,6},{8,7},{9,8},{10,9},{11,1... | collective-permute-start | bytes 9224 | tf_op jit(solution)/shard_map/ppermute | solution.py:21
  450.3 7.9 %collective-permute-start.68 = (f32[1,6,256]{2,1,0:T(8,128)S(1)}, f32[1,6,256]{2,1,0:T(8,128)S(1)}, u32[]{:S(2)}, u32[]{:S(2)}) collective-permute-start(f32[1,6,256]{2,1,0:T(8,128)S(1)} %get-tuple-element.517), channel_id=1, source_target_pairs={{1,0},{2,1},{3,2},{4,3},{5,4},{6,5},{7,6},{8,7},{9,8},{10,9},{11,1... | collective-permute-start | bytes 18440 | tf_op jit(solution)/shard_map/ppermute | solution.py:21
  458.7 8.9 %collective-permute-done.67 = f32[1,6,256]{2,1,0:T(8,128)S(1)} collective-permute-done((f32[1,6,256]{2,1,0:T(8,128)S(1)}, f32[1,6,256]{2,1,0:T(8,128)S(1)}, u32[]{:S(2)}, u32[]{:S(2)}) %collective-permute-start.67) | collective-permute-done | bytes 6176 | tf_op jit(solution)/shard_map/ppermute | solution.py:20
  469.3 7.7 %collective-permute-start.70 = (bf16[6,256,1]{1,0,2:T(8,128)(2,1)S(1)}, bf16[6,256,1]{1,0,2:T(8,128)(2,1)S(1)}, u32[]{:S(2)}, u32[]{:S(2)}) collective-permute-start(bf16[6,256,1]{1,0,2:T(8,128)(2,1)S(1)} %get-tuple-element.660), channel_id=1, source_target_pairs={{1,0},{2,1},{3,2},{4,3},{5,4},{6,5},{7,6},{8,7},{9,8},{10,9},{11,1... | collective-permute-start | bytes 9224 | tf_op jit(solution)/shard_map/ppermute | solution.py:21
  479.6 8.2 %collective-permute-start.72 = (bf16[6,256,1]{1,0,2:T(8,128)(2,1)S(1)}, bf16[6,256,1]{1,0,2:T(8,128)(2,1)S(1)}, u32[]{:S(2)}, u32[]{:S(2)}) collective-permute-start(bf16[6,256,1]{1,0,2:T(8,128)(2,1)S(1)} %get-tuple-element.658), channel_id=1, source_target_pairs={{1,0},{2,1},{3,2},{4,3},{5,4},{6,5},{7,6},{8,7},{9,8},{10,9},{11,1... | collective-permute-start | bytes 9224 | tf_op jit(solution)/shard_map/ppermute | solution.py:21
  490.5 8.1 %collective-permute-start.74 = (f32[1,6,256]{2,1,0:T(8,128)S(1)}, f32[1,6,256]{2,1,0:T(8,128)S(1)}, u32[]{:S(2)}, u32[]{:S(2)}) collective-permute-start(f32[1,6,256]{2,1,0:T(8,128)S(1)} %get-tuple-element.505), channel_id=1, source_target_pairs={{1,0},{2,1},{3,2},{4,3},{5,4},{6,5},{7,6},{8,7},{9,8},{10,9},{11,1... | collective-permute-start | bytes 18440 | tf_op jit(solution)/shard_map/ppermute | solution.py:21
  499.0 8.9 %collective-permute-done.73 = f32[1,6,256]{2,1,0:T(8,128)S(1)} collective-permute-done((f32[1,6,256]{2,1,0:T(8,128)S(1)}, f32[1,6,256]{2,1,0:T(8,128)S(1)}, u32[]{:S(2)}, u32[]{:S(2)}) %collective-permute-start.73) | collective-permute-done | bytes 6176 | tf_op jit(solution)/shard_map/ppermute | solution.py:20
  518.4 7.7 %collective-permute-start.77 = (bf16[6,256,1]{1,0,2:T(8,128)(2,1)S(1)}, bf16[6,256,1]{1,0,2:T(8,128)(2,1)S(1)}, u32[]{:S(2)}, u32[]{:S(2)}) collective-permute-start(bf16[6,256,1]{1,0,2:T(8,128)(2,1)S(1)} %get-tuple-element.654), channel_id=1, source_target_pairs={{1,0},{2,1},{3,2},{4,3},{5,4},{6,5},{7,6},{8,7},{9,8},{10,9},{11,1... | collective-permute-start | bytes 9224 | tf_op jit(solution)/shard_map/ppermute | solution.py:21
  528.7 7.8 %collective-permute-start.79 = (bf16[6,256,1]{1,0,2:T(8,128)(2,1)S(1)}, bf16[6,256,1]{1,0,2:T(8,128)(2,1)S(1)}, u32[]{:S(2)}, u32[]{:S(2)}) collective-permute-start(bf16[6,256,1]{1,0,2:T(8,128)(2,1)S(1)} %get-tuple-element.652), channel_id=1, source_target_pairs={{1,0},{2,1},{3,2},{4,3},{5,4},{6,5},{7,6},{8,7},{9,8},{10,9},{11,1... | collective-permute-start | bytes 9224 | tf_op jit(solution)/shard_map/ppermute | solution.py:21
  539.3 7.9 %collective-permute-start.81 = (f32[1,6,256]{2,1,0:T(8,128)S(1)}, f32[1,6,256]{2,1,0:T(8,128)S(1)}, u32[]{:S(2)}, u32[]{:S(2)}) collective-permute-start(f32[1,6,256]{2,1,0:T(8,128)S(1)} %get-tuple-element.495), channel_id=1, source_target_pairs={{1,0},{2,1},{3,2},{4,3},{5,4},{6,5},{7,6},{8,7},{9,8},{10,9},{11,1... | collective-permute-start | bytes 18440 | tf_op jit(solution)/shard_map/ppermute | solution.py:21
  547.7 8.9 %collective-permute-done.80 = f32[1,6,256]{2,1,0:T(8,128)S(1)} collective-permute-done((f32[1,6,256]{2,1,0:T(8,128)S(1)}, f32[1,6,256]{2,1,0:T(8,128)S(1)}, u32[]{:S(2)}, u32[]{:S(2)}) %collective-permute-start.80) | collective-permute-done | bytes 6176 | tf_op jit(solution)/shard_map/ppermute | solution.py:20
  558.5 7.7 %collective-permute-start.83 = (bf16[6,256,1]{1,0,2:T(8,128)(2,1)S(1)}, bf16[6,256,1]{1,0,2:T(8,128)(2,1)S(1)}, u32[]{:S(2)}, u32[]{:S(2)}) collective-permute-start(bf16[6,256,1]{1,0,2:T(8,128)(2,1)S(1)} %get-tuple-element.650), channel_id=1, source_target_pairs={{1,0},{2,1},{3,2},{4,3},{5,4},{6,5},{7,6},{8,7},{9,8},{10,9},{11,1... | collective-permute-start | bytes 9224 | tf_op jit(solution)/shard_map/ppermute | solution.py:21
  568.9 7.8 %collective-permute-start.85 = (bf16[6,256,1]{1,0,2:T(8,128)(2,1)S(1)}, bf16[6,256,1]{1,0,2:T(8,128)(2,1)S(1)}, u32[]{:S(2)}, u32[]{:S(2)}) collective-permute-start(bf16[6,256,1]{1,0,2:T(8,128)(2,1)S(1)} %get-tuple-element.648), channel_id=1, source_target_pairs={{1,0},{2,1},{3,2},{4,3},{5,4},{6,5},{7,6},{8,7},{9,8},{10,9},{11,1... | collective-permute-start | bytes 9224 | tf_op jit(solution)/shard_map/ppermute | solution.py:21
  579.5 7.9 %collective-permute-start.87 = (f32[1,6,256]{2,1,0:T(8,128)S(1)}, f32[1,6,256]{2,1,0:T(8,128)S(1)}, u32[]{:S(2)}, u32[]{:S(2)}) collective-permute-start(f32[1,6,256]{2,1,0:T(8,128)S(1)} %get-tuple-element.483), channel_id=1, source_target_pairs={{1,0},{2,1},{3,2},{4,3},{5,4},{6,5},{7,6},{8,7},{9,8},{10,9},{11,1... | collective-permute-start | bytes 18440 | tf_op jit(solution)/shard_map/ppermute | solution.py:21
  587.9 8.9 %collective-permute-done.86 = f32[1,6,256]{2,1,0:T(8,128)S(1)} collective-permute-done((f32[1,6,256]{2,1,0:T(8,128)S(1)}, f32[1,6,256]{2,1,0:T(8,128)S(1)}, u32[]{:S(2)}, u32[]{:S(2)}) %collective-permute-start.86) | collective-permute-done | bytes 6176 | tf_op jit(solution)/shard_map/ppermute | solution.py:20
  598.5 7.7 %collective-permute-start.89 = (bf16[6,256,1]{1,0,2:T(8,128)(2,1)S(1)}, bf16[6,256,1]{1,0,2:T(8,128)(2,1)S(1)}, u32[]{:S(2)}, u32[]{:S(2)}) collective-permute-start(bf16[6,256,1]{1,0,2:T(8,128)(2,1)S(1)} %get-tuple-element.646), channel_id=1, source_target_pairs={{1,0},{2,1},{3,2},{4,3},{5,4},{6,5},{7,6},{8,7},{9,8},{10,9},{11,1... | collective-permute-start | bytes 9224 | tf_op jit(solution)/shard_map/ppermute | solution.py:21
  608.8 7.8 %collective-permute-start.91 = (bf16[6,256,1]{1,0,2:T(8,128)(2,1)S(1)}, bf16[6,256,1]{1,0,2:T(8,128)(2,1)S(1)}, u32[]{:S(2)}, u32[]{:S(2)}) collective-permute-start(bf16[6,256,1]{1,0,2:T(8,128)(2,1)S(1)} %get-tuple-element.644), channel_id=1, source_target_pairs={{1,0},{2,1},{3,2},{4,3},{5,4},{6,5},{7,6},{8,7},{9,8},{10,9},{11,1... | collective-permute-start | bytes 9224 | tf_op jit(solution)/shard_map/ppermute | solution.py:21
  619.5 7.9 %collective-permute-start.93 = (f32[1,6,256]{2,1,0:T(8,128)S(1)}, f32[1,6,256]{2,1,0:T(8,128)S(1)}, u32[]{:S(2)}, u32[]{:S(2)}) collective-permute-start(f32[1,6,256]{2,1,0:T(8,128)S(1)} %get-tuple-element.471), channel_id=1, source_target_pairs={{1,0},{2,1},{3,2},{4,3},{5,4},{6,5},{7,6},{8,7},{9,8},{10,9},{11,1... | collective-permute-start | bytes 18440 | tf_op jit(solution)/shard_map/ppermute | solution.py:21
  628.0 8.9 %collective-permute-done.92 = f32[1,6,256]{2,1,0:T(8,128)S(1)} collective-permute-done((f32[1,6,256]{2,1,0:T(8,128)S(1)}, f32[1,6,256]{2,1,0:T(8,128)S(1)}, u32[]{:S(2)}, u32[]{:S(2)}) %collective-permute-start.92) | collective-permute-done | bytes 6176 | tf_op jit(solution)/shard_map/ppermute | solution.py:20
  638.6 7.7 %collective-permute-start.95 = (bf16[6,256,1]{1,0,2:T(8,128)(2,1)S(1)}, bf16[6,256,1]{1,0,2:T(8,128)(2,1)S(1)}, u32[]{:S(2)}, u32[]{:S(2)}) collective-permute-start(bf16[6,256,1]{1,0,2:T(8,128)(2,1)S(1)} %get-tuple-element.642), channel_id=1, source_target_pairs={{1,0},{2,1},{3,2},{4,3},{5,4},{6,5},{7,6},{8,7},{9,8},{10,9},{11,1... | collective-permute-start | bytes 9224 | tf_op jit(solution)/shard_map/ppermute | solution.py:21
  648.9 7.8 %collective-permute-start.97 = (bf16[6,256,1]{1,0,2:T(8,128)(2,1)S(1)}, bf16[6,256,1]{1,0,2:T(8,128)(2,1)S(1)}, u32[]{:S(2)}, u32[]{:S(2)}) collective-permute-start(bf16[6,256,1]{1,0,2:T(8,128)(2,1)S(1)} %get-tuple-element.640), channel_id=1, source_target_pairs={{1,0},{2,1},{3,2},{4,3},{5,4},{6,5},{7,6},{8,7},{9,8},{10,9},{11,1... | collective-permute-start | bytes 9224 | tf_op jit(solution)/shard_map/ppermute | solution.py:21
  659.6 7.9 %collective-permute-start.99 = (f32[1,6,256]{2,1,0:T(8,128)S(1)}, f32[1,6,256]{2,1,0:T(8,128)S(1)}, u32[]{:S(2)}, u32[]{:S(2)}) collective-permute-start(f32[1,6,256]{2,1,0:T(8,128)S(1)} %get-tuple-element.459), channel_id=1, source_target_pairs={{1,0},{2,1},{3,2},{4,3},{5,4},{6,5},{7,6},{8,7},{9,8},{10,9},{11,1... | collective-permute-start | bytes 18440 | tf_op jit(solution)/shard_map/ppermute | solution.py:21
  668.0 8.9 %collective-permute-done.98 = f32[1,6,256]{2,1,0:T(8,128)S(1)} collective-permute-done((f32[1,6,256]{2,1,0:T(8,128)S(1)}, f32[1,6,256]{2,1,0:T(8,128)S(1)}, u32[]{:S(2)}, u32[]{:S(2)}) %collective-permute-start.98) | collective-permute-done | bytes 6176 | tf_op jit(solution)/shard_map/ppermute | solution.py:20
  (428 shorter events, 157.9 us)
Async XLA Ops:
  0.0 20.4 %collective-permute-start.1 = (bf16[6,256,1]{1,0,2:T(8,128)(2,1)S(1)}, bf16[6,256,1]{1,0,2:T(8,128)(2,1)S(1)}, u32[]{:S(2)}, u32[]{:S(2)}) collective-permute-start(bf16[6,256,1]{1,0,2:T(8,128)(2,1)S(1)} %slice.1602), channel_id=1, source_target_pairs={{1,0},{2,1},{3,2},{4,3},{5,4},{6,5},{7,6},{8,7},{9,8},{10,9},{11,1... | collective-permute-start | bytes 9224 | tf_op jit(solution)/shard_map/ppermute | solution.py:21
  8.1 12.3 %collective-permute-start = (bf16[6,256,1]{1,0,2:T(8,128)(2,1)S(1)}, bf16[6,256,1]{1,0,2:T(8,128)(2,1)S(1)}, u32[]{:S(2)}, u32[]{:S(2)}) collective-permute-start(bf16[6,256,1]{1,0,2:T(8,128)(2,1)S(1)} %slice.1602), channel_id=1, source_target_pairs={{0,1},{1,2},{2,3},{3,4},{4,5},{5,6},{6,7},{7,8},{8,9},{9,10},{10,1... | collective-permute-start | bytes 9224 | tf_op jit(solution)/shard_map/ppermute | solution.py:20
  9.8 9.6 %collective-permute-start.2 = (f32[1,256]{1,0:T(1,128)}, f32[1,256]{1,0:T(1,128)}, u32[]{:S(2)}, u32[]{:S(2)}) collective-permute-start(f32[1,256]{1,0:T(1,128)} %bitcast.112), channel_id=1, source_target_pairs={{31,0},{0,1},{1,2},{2,3},{3,4},{4,5},{5,6},{6,7},{7,8},{8,9},{9,10... | collective-permute-start | bytes 3080 | tf_op jit(solution)/shard_map/ppermute | solution.py:29
  21.1 9.4 %collective-permute-start.3 = (bf16[6,256,1]{1,0,2:T(8,128)(2,1)S(1)}, bf16[6,256,1]{1,0,2:T(8,128)(2,1)S(1)}, u32[]{:S(2)}, u32[]{:S(2)}) collective-permute-start(bf16[6,256,1]{1,0,2:T(8,128)(2,1)S(1)} %get-tuple-element.705), channel_id=1, source_target_pairs={{0,1},{1,2},{2,3},{3,4},{4,5},{5,6},{6,7},{7,8},{8,9},{9,10},{10,1... | collective-permute-start | bytes 9224 | tf_op jit(solution)/shard_map/ppermute | solution.py:20
  31.7 17.2 %collective-permute-start.6 = (f32[1,6,256]{2,1,0:T(8,128)S(1)}, f32[1,6,256]{2,1,0:T(8,128)S(1)}, u32[]{:S(2)}, u32[]{:S(2)}) collective-permute-start(f32[1,6,256]{2,1,0:T(8,128)S(1)} %get-tuple-element.633), channel_id=1, source_target_pairs={{1,0},{2,1},{3,2},{4,3},{5,4},{6,5},{7,6},{8,7},{9,8},{10,9},{11,1... | collective-permute-start | bytes 18440 | tf_op jit(solution)/shard_map/ppermute | solution.py:21
  39.5 9.4 %collective-permute-start.5 = (f32[1,6,256]{2,1,0:T(8,128)S(1)}, f32[1,6,256]{2,1,0:T(8,128)S(1)}, u32[]{:S(2)}, u32[]{:S(2)}) collective-permute-start(f32[1,6,256]{2,1,0:T(8,128)S(1)} %get-tuple-element.634), channel_id=1, source_target_pairs={{0,1},{1,2},{2,3},{3,4},{4,5},{5,6},{6,7},{7,8},{8,9},{9,10},{10,1... | collective-permute-start | bytes 18440 | tf_op jit(solution)/shard_map/ppermute | solution.py:20
  50.6 9.4 %collective-permute-start.7 = (bf16[6,256,1]{1,0,2:T(8,128)(2,1)S(1)}, bf16[6,256,1]{1,0,2:T(8,128)(2,1)S(1)}, u32[]{:S(2)}, u32[]{:S(2)}) collective-permute-start(bf16[6,256,1]{1,0,2:T(8,128)(2,1)S(1)} %get-tuple-element.703), channel_id=1, source_target_pairs={{0,1},{1,2},{2,3},{3,4},{4,5},{5,6},{6,7},{7,8},{8,9},{9,10},{10,1... | collective-permute-start | bytes 9224 | tf_op jit(solution)/shard_map/ppermute | solution.py:20
  60.9 9.4 %collective-permute-start.9 = (bf16[6,256,1]{1,0,2:T(8,128)(2,1)S(1)}, bf16[6,256,1]{1,0,2:T(8,128)(2,1)S(1)}, u32[]{:S(2)}, u32[]{:S(2)}) collective-permute-start(bf16[6,256,1]{1,0,2:T(8,128)(2,1)S(1)} %get-tuple-element.701), channel_id=1, source_target_pairs={{0,1},{1,2},{2,3},{3,4},{4,5},{5,6},{6,7},{7,8},{8,9},{9,10},{10,1... | collective-permute-start | bytes 9224 | tf_op jit(solution)/shard_map/ppermute | solution.py:20
  61.0 9.6 %collective-permute-start.10 = (bf16[6,256,1]{1,0,2:T(8,128)(2,1)S(1)}, bf16[6,256,1]{1,0,2:T(8,128)(2,1)S(1)}, u32[]{:S(2)}, u32[]{:S(2)}) collective-permute-start(bf16[6,256,1]{1,0,2:T(8,128)(2,1)S(1)} %get-tuple-element.702), channel_id=1, source_target_pairs={{1,0},{2,1},{3,2},{4,3},{5,4},{6,5},{7,6},{8,7},{9,8},{10,9},{11,1... | collective-permute-start | bytes 9224 | tf_op jit(solution)/shard_map/ppermute | solution.py:21
  71.9 17.5 %collective-permute-start.12 = (f32[1,6,256]{2,1,0:T(8,128)S(1)}, f32[1,6,256]{2,1,0:T(8,128)S(1)}, u32[]{:S(2)}, u32[]{:S(2)}) collective-permute-start(f32[1,6,256]{2,1,0:T(8,128)S(1)} %get-tuple-element.621), channel_id=1, source_target_pairs={{1,0},{2,1},{3,2},{4,3},{5,4},{6,5},{7,6},{8,7},{9,8},{10,9},{11,1... | collective-permute-start | bytes 18440 | tf_op jit(solution)/shard_map/ppermute | solution.py:21
  91.0 9.4 %collective-permute-start.13 = (bf16[6,256,1]{1,0,2:T(8,128)(2,1)S(1)}, bf16[6,256,1]{1,0,2:T(8,128)(2,1)S(1)}, u32[]{:S(2)}, u32[]{:S(2)}) collective-permute-start(bf16[6,256,1]{1,0,2:T(8,128)(2,1)S(1)} %get-tuple-element.699), channel_id=1, source_target_pairs={{0,1},{1,2},{2,3},{3,4},{4,5},{5,6},{6,7},{7,8},{8,9},{9,10},{10,1... | collective-permute-start | bytes 9224 | tf_op jit(solution)/shard_map/ppermute | solution.py:20
  101.3 9.4 %collective-permute-start.15 = (bf16[6,256,1]{1,0,2:T(8,128)(2,1)S(1)}, bf16[6,256,1]{1,0,2:T(8,128)(2,1)S(1)}, u32[]{:S(2)}, u32[]{:S(2)}) collective-permute-start(bf16[6,256,1]{1,0,2:T(8,128)(2,1)S(1)} %get-tuple-element.697), channel_id=1, source_target_pairs={{0,1},{1,2},{2,3},{3,4},{4,5},{5,6},{6,7},{7,8},{8,9},{9,10},{10,1... | collective-permute-start | bytes 9224 | tf_op jit(solution)/shard_map/ppermute | solution.py:20
  112.0 17.3 %collective-permute-start.18 = (f32[1,6,256]{2,1,0:T(8,128)S(1)}, f32[1,6,256]{2,1,0:T(8,128)S(1)}, u32[]{:S(2)}, u32[]{:S(2)}) collective-permute-start(f32[1,6,256]{2,1,0:T(8,128)S(1)} %get-tuple-element.609), channel_id=1, source_target_pairs={{1,0},{2,1},{3,2},{4,3},{5,4},{6,5},{7,6},{8,7},{9,8},{10,9},{11,1... | collective-permute-start | bytes 18440 | tf_op jit(solution)/shard_map/ppermute | solution.py:21
  119.9 9.4 %collective-permute-start.17 = (f32[1,6,256]{2,1,0:T(8,128)S(1)}, f32[1,6,256]{2,1,0:T(8,128)S(1)}, u32[]{:S(2)}, u32[]{:S(2)}) collective-permute-start(f32[1,6,256]{2,1,0:T(8,128)S(1)} %get-tuple-element.610), channel_id=1, source_target_pairs={{0,1},{1,2},{2,3},{3,4},{4,5},{5,6},{6,7},{7,8},{8,9},{9,10},{10,1... | collective-permute-start | bytes 18440 | tf_op jit(solution)/shard_map/ppermute | solution.py:20
  130.9 9.4 %collective-permute-start.19 = (bf16[6,256,1]{1,0,2:T(8,128)(2,1)S(1)}, bf16[6,256,1]{1,0,2:T(8,128)(2,1)S(1)}, u32[]{:S(2)}, u32[]{:S(2)}) collective-permute-start(bf16[6,256,1]{1,0,2:T(8,128)(2,1)S(1)} %get-tuple-element.695), channel_id=1, source_target_pairs={{0,1},{1,2},{2,3},{3,4},{4,5},{5,6},{6,7},{7,8},{8,9},{9,10},{10,1... | collective-permute-start | bytes 9224 | tf_op jit(solution)/shard_map/ppermute | solution.py:20
  141.3 9.6 %collective-permute-start.21 = (bf16[6,256,1]{1,0,2:T(8,128)(2,1)S(1)}, bf16[6,256,1]{1,0,2:T(8,128)(2,1)S(1)}, u32[]{:S(2)}, u32[]{:S(2)}) collective-permute-start(bf16[6,256,1]{1,0,2:T(8,128)(2,1)S(1)} %get-tuple-element.693), channel_id=1, source_target_pairs={{0,1},{1,2},{2,3},{3,4},{4,5},{5,6},{6,7},{7,8},{8,9},{9,10},{10,1... | collective-permute-start | bytes 9224 | tf_op jit(solution)/shard_map/ppermute | solution.py:20
  141.4 9.5 %collective-permute-start.22 = (bf16[6,256,1]{1,0,2:T(8,128)(2,1)S(1)}, bf16[6,256,1]{1,0,2:T(8,128)(2,1)S(1)}, u32[]{:S(2)}, u32[]{:S(2)}) collective-permute-start(bf16[6,256,1]{1,0,2:T(8,128)(2,1)S(1)} %get-tuple-element.694), channel_id=1, source_target_pairs={{1,0},{2,1},{3,2},{4,3},{5,4},{6,5},{7,6},{8,7},{9,8},{10,9},{11,1... | collective-permute-start | bytes 9224 | tf_op jit(solution)/shard_map/ppermute | solution.py:21
  152.2 17.3 %collective-permute-start.24 = (f32[1,6,256]{2,1,0:T(8,128)S(1)}, f32[1,6,256]{2,1,0:T(8,128)S(1)}, u32[]{:S(2)}, u32[]{:S(2)}) collective-permute-start(f32[1,6,256]{2,1,0:T(8,128)S(1)} %get-tuple-element.597), channel_id=1, source_target_pairs={{1,0},{2,1},{3,2},{4,3},{5,4},{6,5},{7,6},{8,7},{9,8},{10,9},{11,1... | collective-permute-start | bytes 18440 | tf_op jit(solution)/shard_map/ppermute | solution.py:21
  179.8 9.4 %collective-permute-start.26 = (bf16[6,256,1]{1,0,2:T(8,128)(2,1)S(1)}, bf16[6,256,1]{1,0,2:T(8,128)(2,1)S(1)}, u32[]{:S(2)}, u32[]{:S(2)}) collective-permute-start(bf16[6,256,1]{1,0,2:T(8,128)(2,1)S(1)} %get-tuple-element.689), channel_id=1, source_target_pairs={{0,1},{1,2},{2,3},{3,4},{4,5},{5,6},{6,7},{7,8},{8,9},{9,10},{10,1... | collective-permute-start | bytes 9224 | tf_op jit(solution)/shard_map/ppermute | solution.py:20
  190.2 9.4 %collective-permute-start.28 = (bf16[6,256,1]{1,0,2:T(8,128)(2,1)S(1)}, bf16[6,256,1]{1,0,2:T(8,128)(2,1)S(1)}, u32[]{:S(2)}, u32[]{:S(2)}) collective-permute-start(bf16[6,256,1]{1,0,2:T(8,128)(2,1)S(1)} %get-tuple-element.687), channel_id=1, source_target_pairs={{0,1},{1,2},{2,3},{3,4},{4,5},{5,6},{6,7},{7,8},{8,9},{9,10},{10,1... | collective-permute-start | bytes 9224 | tf_op jit(solution)/shard_map/ppermute | solution.py:20
  200.9 17.5 %collective-permute-start.31 = (f32[1,6,256]{2,1,0:T(8,128)S(1)}, f32[1,6,256]{2,1,0:T(8,128)S(1)}, u32[]{:S(2)}, u32[]{:S(2)}) collective-permute-start(f32[1,6,256]{2,1,0:T(8,128)S(1)} %get-tuple-element.587), channel_id=1, source_target_pairs={{1,0},{2,1},{3,2},{4,3},{5,4},{6,5},{7,6},{8,7},{9,8},{10,9},{11,1... | collective-permute-start | bytes 18440 | tf_op jit(solution)/shard_map/ppermute | solution.py:21
  208.8 9.6 %collective-permute-start.30 = (f32[1,6,256]{2,1,0:T(8,128)S(1)}, f32[1,6,256]{2,1,0:T(8,128)S(1)}, u32[]{:S(2)}, u32[]{:S(2)}) collective-permute-start(f32[1,6,256]{2,1,0:T(8,128)S(1)} %get-tuple-element.588), channel_id=1, source_target_pairs={{0,1},{1,2},{2,3},{3,4},{4,5},{5,6},{6,7},{7,8},{8,9},{9,10},{10,1... | collective-permute-start | bytes 18440 | tf_op jit(solution)/shard_map/ppermute | solution.py:20
  220.0 9.4 %collective-permute-start.32 = (bf16[6,256,1]{1,0,2:T(8,128)(2,1)S(1)}, bf16[6,256,1]{1,0,2:T(8,128)(2,1)S(1)}, u32[]{:S(2)}, u32[]{:S(2)}) collective-permute-start(bf16[6,256,1]{1,0,2:T(8,128)(2,1)S(1)} %get-tuple-element.685), channel_id=1, source_target_pairs={{0,1},{1,2},{2,3},{3,4},{4,5},{5,6},{6,7},{7,8},{8,9},{9,10},{10,1... | collective-permute-start | bytes 9224 | tf_op jit(solution)/shard_map/ppermute | solution.py:20
  230.3 9.4 %collective-permute-start.34 = (bf16[6,256,1]{1,0,2:T(8,128)(2,1)S(1)}, bf16[6,256,1]{1,0,2:T(8,128)(2,1)S(1)}, u32[]{:S(2)}, u32[]{:S(2)}) collective-permute-start(bf16[6,256,1]{1,0,2:T(8,128)(2,1)S(1)} %get-tuple-element.683), channel_id=1, source_target_pairs={{0,1},{1,2},{2,3},{3,4},{4,5},{5,6},{6,7},{7,8},{8,9},{9,10},{10,1... | collective-permute-start | bytes 9224 | tf_op jit(solution)/shard_map/ppermute | solution.py:20
  241.0 17.3 %collective-permute-start.37 = (f32[1,6,256]{2,1,0:T(8,128)S(1)}, f32[1,6,256]{2,1,0:T(8,128)S(1)}, u32[]{:S(2)}, u32[]{:S(2)}) collective-permute-start(f32[1,6,256]{2,1,0:T(8,128)S(1)} %get-tuple-element.575), channel_id=1, source_target_pairs={{1,0},{2,1},{3,2},{4,3},{5,4},{6,5},{7,6},{8,7},{9,8},{10,9},{11,1... | collective-permute-start | bytes 18440 | tf_op jit(solution)/shard_map/ppermute | solution.py:21
  248.9 9.4 %collective-permute-start.36 = (f32[1,6,256]{2,1,0:T(8,128)S(1)}, f32[1,6,256]{2,1,0:T(8,128)S(1)}, u32[]{:S(2)}, u32[]{:S(2)}) collective-permute-start(f32[1,6,256]{2,1,0:T(8,128)S(1)} %get-tuple-element.576), channel_id=1, source_target_pairs={{0,1},{1,2},{2,3},{3,4},{4,5},{5,6},{6,7},{7,8},{8,9},{9,10},{10,1... | collective-permute-start | bytes 18440 | tf_op jit(solution)/shard_map/ppermute | solution.py:20
  259.9 9.4 %collective-permute-start.38 = (bf16[6,256,1]{1,0,2:T(8,128)(2,1)S(1)}, bf16[6,256,1]{1,0,2:T(8,128)(2,1)S(1)}, u32[]{:S(2)}, u32[]{:S(2)}) collective-permute-start(bf16[6,256,1]{1,0,2:T(8,128)(2,1)S(1)} %get-tuple-element.681), channel_id=1, source_target_pairs={{0,1},{1,2},{2,3},{3,4},{4,5},{5,6},{6,7},{7,8},{8,9},{9,10},{10,1... | collective-permute-start | bytes 9224 | tf_op jit(solution)/shard_map/ppermute | solution.py:20
  270.3 9.4 %collective-permute-start.40 = (bf16[6,256,1]{1,0,2:T(8,128)(2,1)S(1)}, bf16[6,256,1]{1,0,2:T(8,128)(2,1)S(1)}, u32[]{:S(2)}, u32[]{:S(2)}) collective-permute-start(bf16[6,256,1]{1,0,2:T(8,128)(2,1)S(1)} %get-tuple-element.679), channel_id=1, source_target_pairs={{0,1},{1,2},{2,3},{3,4},{4,5},{5,6},{6,7},{7,8},{8,9},{9,10},{10,1... | collective-permute-start | bytes 9224 | tf_op jit(solution)/shard_map/ppermute | solution.py:20
  270.3 9.5 %collective-permute-start.41 = (bf16[6,256,1]{1,0,2:T(8,128)(2,1)S(1)}, bf16[6,256,1]{1,0,2:T(8,128)(2,1)S(1)}, u32[]{:S(2)}, u32[]{:S(2)}) collective-permute-start(bf16[6,256,1]{1,0,2:T(8,128)(2,1)S(1)} %get-tuple-element.680), channel_id=1, source_target_pairs={{1,0},{2,1},{3,2},{4,3},{5,4},{6,5},{7,6},{8,7},{9,8},{10,9},{11,1... | collective-permute-start | bytes 9224 | tf_op jit(solution)/shard_map/ppermute | solution.py:21
  281.2 17.5 %collective-permute-start.43 = (f32[1,6,256]{2,1,0:T(8,128)S(1)}, f32[1,6,256]{2,1,0:T(8,128)S(1)}, u32[]{:S(2)}, u32[]{:S(2)}) collective-permute-start(f32[1,6,256]{2,1,0:T(8,128)S(1)} %get-tuple-element.563), channel_id=1, source_target_pairs={{1,0},{2,1},{3,2},{4,3},{5,4},{6,5},{7,6},{8,7},{9,8},{10,9},{11,1... | collective-permute-start | bytes 18440 | tf_op jit(solution)/shard_map/ppermute | solution.py:21
  289.3 9.4 %collective-permute-start.42 = (f32[1,6,256]{2,1,0:T(8,128)S(1)}, f32[1,6,256]{2,1,0:T(8,128)S(1)}, u32[]{:S(2)}, u32[]{:S(2)}) collective-permute-start(f32[1,6,256]{2,1,0:T(8,128)S(1)} %get-tuple-element.564), channel_id=1, source_target_pairs={{0,1},{1,2},{2,3},{3,4},{4,5},{5,6},{6,7},{7,8},{8,9},{9,10},{10,1... | collective-permute-start | bytes 18440 | tf_op jit(solution)/shard_map/ppermute | solution.py:20
  300.3 9.4 %collective-permute-start.44 = (bf16[6,256,1]{1,0,2:T(8,128)(2,1)S(1)}, bf16[6,256,1]{1,0,2:T(8,128)(2,1)S(1)}, u32[]{:S(2)}, u32[]{:S(2)}) collective-permute-start(bf16[6,256,1]{1,0,2:T(8,128)(2,1)S(1)} %get-tuple-element.677), channel_id=1, source_target_pairs={{0,1},{1,2},{2,3},{3,4},{4,5},{5,6},{6,7},{7,8},{8,9},{9,10},{10,1... | collective-permute-start | bytes 9224 | tf_op jit(solution)/shard_map/ppermute | solution.py:20
  310.6 9.4 %collective-permute-start.46 = (bf16[6,256,1]{1,0,2:T(8,128)(2,1)S(1)}, bf16[6,256,1]{1,0,2:T(8,128)(2,1)S(1)}, u32[]{:S(2)}, u32[]{:S(2)}) collective-permute-start(bf16[6,256,1]{1,0,2:T(8,128)(2,1)S(1)} %get-tuple-element.675), channel_id=1, source_target_pairs={{0,1},{1,2},{2,3},{3,4},{4,5},{5,6},{6,7},{7,8},{8,9},{9,10},{10,1... | collective-permute-start | bytes 9224 | tf_op jit(solution)/shard_map/ppermute | solution.py:20
  321.3 17.3 %collective-permute-start.49 = (f32[1,6,256]{2,1,0:T(8,128)S(1)}, f32[1,6,256]{2,1,0:T(8,128)S(1)}, u32[]{:S(2)}, u32[]{:S(2)}) collective-permute-start(f32[1,6,256]{2,1,0:T(8,128)S(1)} %get-tuple-element.551), channel_id=1, source_target_pairs={{1,0},{2,1},{3,2},{4,3},{5,4},{6,5},{7,6},{8,7},{9,8},{10,9},{11,1... | collective-permute-start | bytes 18440 | tf_op jit(solution)/shard_map/ppermute | solution.py:21
  329.2 9.4 %collective-permute-start.48 = (f32[1,6,256]{2,1,0:T(8,128)S(1)}, f32[1,6,256]{2,1,0:T(8,128)S(1)}, u32[]{:S(2)}, u32[]{:S(2)}) collective-permute-start(f32[1,6,256]{2,1,0:T(8,128)S(1)} %get-tuple-element.552), channel_id=1, source_target_pairs={{0,1},{1,2},{2,3},{3,4},{4,5},{5,6},{6,7},{7,8},{8,9},{9,10},{10,1... | collective-permute-start | bytes 18440 | tf_op jit(solution)/shard_map/ppermute | solution.py:20
  349.0 9.4 %collective-permute-start.51 = (bf16[6,256,1]{1,0,2:T(8,128)(2,1)S(1)}, bf16[6,256,1]{1,0,2:T(8,128)(2,1)S(1)}, u32[]{:S(2)}, u32[]{:S(2)}) collective-permute-start(bf16[6,256,1]{1,0,2:T(8,128)(2,1)S(1)} %get-tuple-element.671), channel_id=1, source_target_pairs={{0,1},{1,2},{2,3},{3,4},{4,5},{5,6},{6,7},{7,8},{8,9},{9,10},{10,1... | collective-permute-start | bytes 9224 | tf_op jit(solution)/shard_map/ppermute | solution.py:20
  359.3 9.6 %collective-permute-start.53 = (bf16[6,256,1]{1,0,2:T(8,128)(2,1)S(1)}, bf16[6,256,1]{1,0,2:T(8,128)(2,1)S(1)}, u32[]{:S(2)}, u32[]{:S(2)}) collective-permute-start(bf16[6,256,1]{1,0,2:T(8,128)(2,1)S(1)} %get-tuple-element.669), channel_id=1, source_target_pairs={{0,1},{1,2},{2,3},{3,4},{4,5},{5,6},{6,7},{7,8},{8,9},{9,10},{10,1... | collective-permute-start | bytes 9224 | tf_op jit(solution)/shard_map/ppermute | solution.py:20
  359.4 9.5 %collective-permute-start.54 = (bf16[6,256,1]{1,0,2:T(8,128)(2,1)S(1)}, bf16[6,256,1]{1,0,2:T(8,128)(2,1)S(1)}, u32[]{:S(2)}, u32[]{:S(2)}) collective-permute-start(bf16[6,256,1]{1,0,2:T(8,128)(2,1)S(1)} %get-tuple-element.670), channel_id=1, source_target_pairs={{1,0},{2,1},{3,2},{4,3},{5,4},{6,5},{7,6},{8,7},{9,8},{10,9},{11,1... | collective-permute-start | bytes 9224 | tf_op jit(solution)/shard_map/ppermute | solution.py:21
  370.2 17.3 %collective-permute-start.56 = (f32[1,6,256]{2,1,0:T(8,128)S(1)}, f32[1,6,256]{2,1,0:T(8,128)S(1)}, u32[]{:S(2)}, u32[]{:S(2)}) collective-permute-start(f32[1,6,256]{2,1,0:T(8,128)S(1)} %get-tuple-element.541), channel_id=1, source_target_pairs={{1,0},{2,1},{3,2},{4,3},{5,4},{6,5},{7,6},{8,7},{9,8},{10,9},{11,1... | collective-permute-start | bytes 18440 | tf_op jit(solution)/shard_map/ppermute | solution.py:21
  389.1 9.4 %collective-permute-start.57 = (bf16[6,256,1]{1,0,2:T(8,128)(2,1)S(1)}, bf16[6,256,1]{1,0,2:T(8,128)(2,1)S(1)}, u32[]{:S(2)}, u32[]{:S(2)}) collective-permute-start(bf16[6,256,1]{1,0,2:T(8,128)(2,1)S(1)} %get-tuple-element.667), channel_id=1, source_target_pairs={{0,1},{1,2},{2,3},{3,4},{4,5},{5,6},{6,7},{7,8},{8,9},{9,10},{10,1... | collective-permute-start | bytes 9224 | tf_op jit(solution)/shard_map/ppermute | solution.py:20
  399.5 9.4 %collective-permute-start.59 = (bf16[6,256,1]{1,0,2:T(8,128)(2,1)S(1)}, bf16[6,256,1]{1,0,2:T(8,128)(2,1)S(1)}, u32[]{:S(2)}, u32[]{:S(2)}) collective-permute-start(bf16[6,256,1]{1,0,2:T(8,128)(2,1)S(1)} %get-tuple-element.665), channel_id=1, source_target_pairs={{0,1},{1,2},{2,3},{3,4},{4,5},{5,6},{6,7},{7,8},{8,9},{9,10},{10,1... | collective-permute-start | bytes 9224 | tf_op jit(solution)/shard_map/ppermute | solution.py:20
  410.2 17.5 %collective-permute-start.62 = (f32[1,6,256]{2,1,0:T(8,128)S(1)}, f32[1,6,256]{2,1,0:T(8,128)S(1)}, u32[]{:S(2)}, u32[]{:S(2)}) collective-permute-start(f32[1,6,256]{2,1,0:T(8,128)S(1)} %get-tuple-element.529), channel_id=1, source_target_pairs={{1,0},{2,1},{3,2},{4,3},{5,4},{6,5},{7,6},{8,7},{9,8},{10,9},{11,1... | collective-permute-start | bytes 18440 | tf_op jit(solution)/shard_map/ppermute | solution.py:21
  418.0 9.6 %collective-permute-start.61 = (f32[1,6,256]{2,1,0:T(8,128)S(1)}, f32[1,6,256]{2,1,0:T(8,128)S(1)}, u32[]{:S(2)}, u32[]{:S(2)}) collective-permute-start(f32[1,6,256]{2,1,0:T(8,128)S(1)} %get-tuple-element.530), channel_id=1, source_target_pairs={{0,1},{1,2},{2,3},{3,4},{4,5},{5,6},{6,7},{7,8},{8,9},{9,10},{10,1... | collective-permute-start | bytes 18440 | tf_op jit(solution)/shard_map/ppermute | solution.py:20
  429.2 9.4 %collective-permute-start.63 = (bf16[6,256,1]{1,0,2:T(8,128)(2,1)S(1)}, bf16[6,256,1]{1,0,2:T(8,128)(2,1)S(1)}, u32[]{:S(2)}, u32[]{:S(2)}) collective-permute-start(bf16[6,256,1]{1,0,2:T(8,128)(2,1)S(1)} %get-tuple-element.663), channel_id=1, source_target_pairs={{0,1},{1,2},{2,3},{3,4},{4,5},{5,6},{6,7},{7,8},{8,9},{9,10},{10,1... | collective-permute-start | bytes 9224 | tf_op jit(solution)/shard_map/ppermute | solution.py:20
  439.6 9.4 %collective-permute-start.65 = (bf16[6,256,1]{1,0,2:T(8,128)(2,1)S(1)}, bf16[6,256,1]{1,0,2:T(8,128)(2,1)S(1)}, u32[]{:S(2)}, u32[]{:S(2)}) collective-permute-start(bf16[6,256,1]{1,0,2:T(8,128)(2,1)S(1)} %get-tuple-element.661), channel_id=1, source_target_pairs={{0,1},{1,2},{2,3},{3,4},{4,5},{5,6},{6,7},{7,8},{8,9},{9,10},{10,1... | collective-permute-start | bytes 9224 | tf_op jit(solution)/shard_map/ppermute | solution.py:20
  450.3 17.3 %collective-permute-start.68 = (f32[1,6,256]{2,1,0:T(8,128)S(1)}, f32[1,6,256]{2,1,0:T(8,128)S(1)}, u32[]{:S(2)}, u32[]{:S(2)}) collective-permute-start(f32[1,6,256]{2,1,0:T(8,128)S(1)} %get-tuple-element.517), channel_id=1, source_target_pairs={{1,0},{2,1},{3,2},{4,3},{5,4},{6,5},{7,6},{8,7},{9,8},{10,9},{11,1... | collective-permute-start | bytes 18440 | tf_op jit(solution)/shard_map/ppermute | solution.py:21
  469.2 9.4 %collective-permute-start.69 = (bf16[6,256,1]{1,0,2:T(8,128)(2,1)S(1)}, bf16[6,256,1]{1,0,2:T(8,128)(2,1)S(1)}, u32[]{:S(2)}, u32[]{:S(2)}) collective-permute-start(bf16[6,256,1]{1,0,2:T(8,128)(2,1)S(1)} %get-tuple-element.659), channel_id=1, source_target_pairs={{0,1},{1,2},{2,3},{3,4},{4,5},{5,6},{6,7},{7,8},{8,9},{9,10},{10,1... | collective-permute-start | bytes 9224 | tf_op jit(solution)/shard_map/ppermute | solution.py:20
  479.5 9.4 %collective-permute-start.71 = (bf16[6,256,1]{1,0,2:T(8,128)(2,1)S(1)}, bf16[6,256,1]{1,0,2:T(8,128)(2,1)S(1)}, u32[]{:S(2)}, u32[]{:S(2)}) collective-permute-start(bf16[6,256,1]{1,0,2:T(8,128)(2,1)S(1)} %get-tuple-element.657), channel_id=1, source_target_pairs={{0,1},{1,2},{2,3},{3,4},{4,5},{5,6},{6,7},{7,8},{8,9},{9,10},{10,1... | collective-permute-start | bytes 9224 | tf_op jit(solution)/shard_map/ppermute | solution.py:20
  479.6 9.5 %collective-permute-start.72 = (bf16[6,256,1]{1,0,2:T(8,128)(2,1)S(1)}, bf16[6,256,1]{1,0,2:T(8,128)(2,1)S(1)}, u32[]{:S(2)}, u32[]{:S(2)}) collective-permute-start(bf16[6,256,1]{1,0,2:T(8,128)(2,1)S(1)} %get-tuple-element.658), channel_id=1, source_target_pairs={{1,0},{2,1},{3,2},{4,3},{5,4},{6,5},{7,6},{8,7},{9,8},{10,9},{11,1... | collective-permute-start | bytes 9224 | tf_op jit(solution)/shard_map/ppermute | solution.py:21
  490.5 17.5 %collective-permute-start.74 = (f32[1,6,256]{2,1,0:T(8,128)S(1)}, f32[1,6,256]{2,1,0:T(8,128)S(1)}, u32[]{:S(2)}, u32[]{:S(2)}) collective-permute-start(f32[1,6,256]{2,1,0:T(8,128)S(1)} %get-tuple-element.505), channel_id=1, source_target_pairs={{1,0},{2,1},{3,2},{4,3},{5,4},{6,5},{7,6},{8,7},{9,8},{10,9},{11,1... | collective-permute-start | bytes 18440 | tf_op jit(solution)/shard_map/ppermute | solution.py:21
  518.3 9.4 %collective-permute-start.76 = (bf16[6,256,1]{1,0,2:T(8,128)(2,1)S(1)}, bf16[6,256,1]{1,0,2:T(8,128)(2,1)S(1)}, u32[]{:S(2)}, u32[]{:S(2)}) collective-permute-start(bf16[6,256,1]{1,0,2:T(8,128)(2,1)S(1)} %get-tuple-element.653), channel_id=1, source_target_pairs={{0,1},{1,2},{2,3},{3,4},{4,5},{5,6},{6,7},{7,8},{8,9},{9,10},{10,1... | collective-permute-start | bytes 9224 | tf_op jit(solution)/shard_map/ppermute | solution.py:20
  528.6 9.4 %collective-permute-start.78 = (bf16[6,256,1]{1,0,2:T(8,128)(2,1)S(1)}, bf16[6,256,1]{1,0,2:T(8,128)(2,1)S(1)}, u32[]{:S(2)}, u32[]{:S(2)}) collective-permute-start(bf16[6,256,1]{1,0,2:T(8,128)(2,1)S(1)} %get-tuple-element.651), channel_id=1, source_target_pairs={{0,1},{1,2},{2,3},{3,4},{4,5},{5,6},{6,7},{7,8},{8,9},{9,10},{10,1... | collective-permute-start | bytes 9224 | tf_op jit(solution)/shard_map/ppermute | solution.py:20
  539.3 17.3 %collective-permute-start.81 = (f32[1,6,256]{2,1,0:T(8,128)S(1)}, f32[1,6,256]{2,1,0:T(8,128)S(1)}, u32[]{:S(2)}, u32[]{:S(2)}) collective-permute-start(f32[1,6,256]{2,1,0:T(8,128)S(1)} %get-tuple-element.495), channel_id=1, source_target_pairs={{1,0},{2,1},{3,2},{4,3},{5,4},{6,5},{7,6},{8,7},{9,8},{10,9},{11,1... | collective-permute-start | bytes 18440 | tf_op jit(solution)/shard_map/ppermute | solution.py:21
  558.2 9.6 %collective-permute-start.82 = (bf16[6,256,1]{1,0,2:T(8,128)(2,1)S(1)}, bf16[6,256,1]{1,0,2:T(8,128)(2,1)S(1)}, u32[]{:S(2)}, u32[]{:S(2)}) collective-permute-start(bf16[6,256,1]{1,0,2:T(8,128)(2,1)S(1)} %get-tuple-element.649), channel_id=1, source_target_pairs={{0,1},{1,2},{2,3},{3,4},{4,5},{5,6},{6,7},{7,8},{8,9},{9,10},{10,1... | collective-permute-start | bytes 9224 | tf_op jit(solution)/shard_map/ppermute | solution.py:20
  568.8 9.4 %collective-permute-start.84 = (bf16[6,256,1]{1,0,2:T(8,128)(2,1)S(1)}, bf16[6,256,1]{1,0,2:T(8,128)(2,1)S(1)}, u32[]{:S(2)}, u32[]{:S(2)}) collective-permute-start(bf16[6,256,1]{1,0,2:T(8,128)(2,1)S(1)} %get-tuple-element.647), channel_id=1, source_target_pairs={{0,1},{1,2},{2,3},{3,4},{4,5},{5,6},{6,7},{7,8},{8,9},{9,10},{10,1... | collective-permute-start | bytes 9224 | tf_op jit(solution)/shard_map/ppermute | solution.py:20
  579.5 17.3 %collective-permute-start.87 = (f32[1,6,256]{2,1,0:T(8,128)S(1)}, f32[1,6,256]{2,1,0:T(8,128)S(1)}, u32[]{:S(2)}, u32[]{:S(2)}) collective-permute-start(f32[1,6,256]{2,1,0:T(8,128)S(1)} %get-tuple-element.483), channel_id=1, source_target_pairs={{1,0},{2,1},{3,2},{4,3},{5,4},{6,5},{7,6},{8,7},{9,8},{10,9},{11,1... | collective-permute-start | bytes 18440 | tf_op jit(solution)/shard_map/ppermute | solution.py:21
  587.4 9.4 %collective-permute-start.86 = (f32[1,6,256]{2,1,0:T(8,128)S(1)}, f32[1,6,256]{2,1,0:T(8,128)S(1)}, u32[]{:S(2)}, u32[]{:S(2)}) collective-permute-start(f32[1,6,256]{2,1,0:T(8,128)S(1)} %get-tuple-element.484), channel_id=1, source_target_pairs={{0,1},{1,2},{2,3},{3,4},{4,5},{5,6},{6,7},{7,8},{8,9},{9,10},{10,1... | collective-permute-start | bytes 18440 | tf_op jit(solution)/shard_map/ppermute | solution.py:20
  598.4 9.4 %collective-permute-start.88 = (bf16[6,256,1]{1,0,2:T(8,128)(2,1)S(1)}, bf16[6,256,1]{1,0,2:T(8,128)(2,1)S(1)}, u32[]{:S(2)}, u32[]{:S(2)}) collective-permute-start(bf16[6,256,1]{1,0,2:T(8,128)(2,1)S(1)} %get-tuple-element.645), channel_id=1, source_target_pairs={{0,1},{1,2},{2,3},{3,4},{4,5},{5,6},{6,7},{7,8},{8,9},{9,10},{10,1... | collective-permute-start | bytes 9224 | tf_op jit(solution)/shard_map/ppermute | solution.py:20
  608.7 9.4 %collective-permute-start.90 = (bf16[6,256,1]{1,0,2:T(8,128)(2,1)S(1)}, bf16[6,256,1]{1,0,2:T(8,128)(2,1)S(1)}, u32[]{:S(2)}, u32[]{:S(2)}) collective-permute-start(bf16[6,256,1]{1,0,2:T(8,128)(2,1)S(1)} %get-tuple-element.643), channel_id=1, source_target_pairs={{0,1},{1,2},{2,3},{3,4},{4,5},{5,6},{6,7},{7,8},{8,9},{9,10},{10,1... | collective-permute-start | bytes 9224 | tf_op jit(solution)/shard_map/ppermute | solution.py:20
  619.5 17.5 %collective-permute-start.93 = (f32[1,6,256]{2,1,0:T(8,128)S(1)}, f32[1,6,256]{2,1,0:T(8,128)S(1)}, u32[]{:S(2)}, u32[]{:S(2)}) collective-permute-start(f32[1,6,256]{2,1,0:T(8,128)S(1)} %get-tuple-element.471), channel_id=1, source_target_pairs={{1,0},{2,1},{3,2},{4,3},{5,4},{6,5},{7,6},{8,7},{9,8},{10,9},{11,1... | collective-permute-start | bytes 18440 | tf_op jit(solution)/shard_map/ppermute | solution.py:21
  627.3 9.6 %collective-permute-start.92 = (f32[1,6,256]{2,1,0:T(8,128)S(1)}, f32[1,6,256]{2,1,0:T(8,128)S(1)}, u32[]{:S(2)}, u32[]{:S(2)}) collective-permute-start(f32[1,6,256]{2,1,0:T(8,128)S(1)} %get-tuple-element.472), channel_id=1, source_target_pairs={{0,1},{1,2},{2,3},{3,4},{4,5},{5,6},{6,7},{7,8},{8,9},{9,10},{10,1... | collective-permute-start | bytes 18440 | tf_op jit(solution)/shard_map/ppermute | solution.py:20
  638.5 9.4 %collective-permute-start.94 = (bf16[6,256,1]{1,0,2:T(8,128)(2,1)S(1)}, bf16[6,256,1]{1,0,2:T(8,128)(2,1)S(1)}, u32[]{:S(2)}, u32[]{:S(2)}) collective-permute-start(bf16[6,256,1]{1,0,2:T(8,128)(2,1)S(1)} %get-tuple-element.641), channel_id=1, source_target_pairs={{0,1},{1,2},{2,3},{3,4},{4,5},{5,6},{6,7},{7,8},{8,9},{9,10},{10,1... | collective-permute-start | bytes 9224 | tf_op jit(solution)/shard_map/ppermute | solution.py:20
  648.9 9.4 %collective-permute-start.96 = (bf16[6,256,1]{1,0,2:T(8,128)(2,1)S(1)}, bf16[6,256,1]{1,0,2:T(8,128)(2,1)S(1)}, u32[]{:S(2)}, u32[]{:S(2)}) collective-permute-start(bf16[6,256,1]{1,0,2:T(8,128)(2,1)S(1)} %get-tuple-element.639), channel_id=1, source_target_pairs={{0,1},{1,2},{2,3},{3,4},{4,5},{5,6},{6,7},{7,8},{8,9},{9,10},{10,1... | collective-permute-start | bytes 9224 | tf_op jit(solution)/shard_map/ppermute | solution.py:20
  659.6 17.3 %collective-permute-start.99 = (f32[1,6,256]{2,1,0:T(8,128)S(1)}, f32[1,6,256]{2,1,0:T(8,128)S(1)}, u32[]{:S(2)}, u32[]{:S(2)}) collective-permute-start(f32[1,6,256]{2,1,0:T(8,128)S(1)} %get-tuple-element.459), channel_id=1, source_target_pairs={{1,0},{2,1},{3,2},{4,3},{5,4},{6,5},{7,6},{8,7},{9,8},{10,9},{11,1... | collective-permute-start | bytes 18440 | tf_op jit(solution)/shard_map/ppermute | solution.py:21
  (40 other events, 358.0 us)
where the time goes:
time: 688 us; the launch traced here: 680 us
  starting transfers between devices  387 us (56%)
  waiting for transfers between devices  202 us (29%)
  other arithmetic  37.6 us (5%)
  local copies, waits for them, and re-layouts  26 us (4%)
  matrix products  25.6 us (4%)
    ppermute x48, starting transfers between devices, with_halo(): after = lax.ppermute(leading, axis, down)  378 us
    ppermute x48, waiting for transfers between devices, with_halo(): before = lax.ppermute(last, axis, up)  177 us
    dot_general x16, matrix products, mix_and_meridional(): jnp.einsum('gf,gab->fab', coupling_now, smoothed, precision=lax.Precision...  25.6 us
    ppermute x3, waiting for transfers between devices, shifted_2(): return lax.ppermute(shard, axis, pairs)  20 us
    slice x47, local copies, waits for them, and re-layouts, north(): return jnp.concatenate([values[..., 1:, :], zero_edge], axis=-2)  16.1 us
  transfers between devices with their start and end apart: 100, of which 54 were waited for; matrix products, arithmetic and copies ran while one was open for 4% of the time, Pallas kernels for 0%

commit v1 on v0

v1 whole, which is shorter than its diff:
```python
import functools

import jax
import jax.numpy as jnp
from jax import lax
from jax.experimental import pallas as pl
from jax.experimental.pallas import tpu as pltpu
from jax.sharding import PartitionSpec as P

OMEGA = 0.4
STEPS = 4
F = 6
HALO = 16
HALF = 64
FRAME = HALF + 2 * HALO
T = 11
BASE = (FRAME - 8 * T) // 2
EXT = {3: 16, 2: 8, 1: 8, 0: 0}
MESH = pl.DeviceIdType.MESH


def strided(t):
    return pl.ds(BASE + t, 8, stride=T)


def body(
    forcing, courant_x, courant_y, faces_x, faces_y, coupling, out,
    nat_f, nat_o, even_odd, tr_f, tr_o, fr, op, cp,
    co, mix, r, x1, x2, adj, edge_out, edge_in, hand_out, hand_in, res, outv,
    load_sem, out_sem, loc_sem, part_send, part_recv, ext_send, ext_recv,
    edge_send, edge_recv, hand_send, hand_recv, res_sem,
):
    tm = lax.axis_index("tm")
    space = lax.axis_index("space")
    n_space = lax.axis_size("space")
    h = lax.rem(tm, 2)
    o = 1 - h
    pair = tm // 2

    def at_space(d):
        return lax.rem(space + d + n_space, n_space)

    partner = (2 * pair + o, space)
    to_east = (2 * pair, at_space(1))
    to_west = (2 * pair + 1, at_space(-1))

    ops_in = (faces_x, faces_y, courant_x, courant_y)
    loads = [pltpu.make_async_copy(ops_in[i].at[0], nat_o.at[i], load_sem.at[i]) for i in range(4)]
    loads.append(pltpu.make_async_copy(coupling.at[0], cp.at[h], load_sem.at[4]))
    loads += [pltpu.make_async_copy(forcing.at[0, k], nat_f.at[k], load_sem.at[5 + k]) for k in range(STEPS)]
    for i in (0, 1, 2, 3, 4, 8, 7, 6, 5):
        loads[i].start()

    barrier = pltpu.get_barrier_semaphore()
    count = 0
    for d in (-1, 0, 1):
        for j in range(4):
            if d == 0 and j == 0:
                continue
            other = lax.rem(tm + j, 4)
            pl.semaphore_signal(barrier, inc=1, device_id=(other, at_space(d)), device_id_type=MESH)
            count += 1

    def views(c):
        if c == STEPS:
            return tr_o, (lambda slot: op.at[slot]), HALO
        return tr_f.at[c], (lambda slot: fr.at[slot, c]), EXT[c]

    def own_copy(c):
        src, dst, _ = views(c)
        return pltpu.make_async_copy(
            src.at[:, :, pl.ds(pl.multiple_of(48 * h, 16), 80)],
            dst(h).at[:, :, pl.ds(pl.multiple_of(16 * o, 16), 80)],
            loc_sem.at[c],
        )

    def partner_copy(c):
        src, dst, _ = views(c)
        return pltpu.make_async_remote_copy(
            src_ref=src.at[:, :, pl.ds(pl.multiple_of(48 * o, 16), 80)],
            dst_ref=dst(h).at[:, :, pl.ds(pl.multiple_of(16 * h, 16), 80)],
            send_sem=part_send.at[c], recv_sem=part_recv.at[c],
            device_id=partner, device_id_type=MESH,
        )

    def partner_arrival(c):
        src, dst, _ = views(c)
        return pltpu.make_async_remote_copy(
            src_ref=src.at[:, :, pl.ds(pl.multiple_of(48 * h, 16), 80)],
            dst_ref=dst(o).at[:, :, pl.ds(pl.multiple_of(16 * o, 16), 80)],
            send_sem=part_send.at[c], recv_sem=part_recv.at[c],
            device_id=partner, device_id_type=MESH,
        )

    def ext_copies(c):
        src, dst, n = views(c)
        if n == 0:
            return []
        east = pltpu.make_async_remote_copy(
            src_ref=src.at[:, :, pl.ds(128 - n, n)],
            dst_ref=dst(h).at[:, :, pl.ds(HALO - n, n)],
            send_sem=ext_send.at[0, c], recv_sem=ext_recv.at[h, c],
            device_id=to_east, device_id_type=MESH,
        )
        west = pltpu.make_async_remote_copy(
            src_ref=src.at[:, :, pl.ds(0, n)],
            dst_ref=dst(h).at[:, :, pl.ds(HALO + HALF, n)],
            send_sem=ext_send.at[1, c], recv_sem=ext_recv.at[h, c],
            device_id=to_west, device_id_type=MESH,
        )
        return [east, west]

    def ext_arrival(slot, c):
        src, dst, n = views(c)
        start = pl.multiple_of((HALO - n) * o + (HALO + HALF) * h, 8)
        return pltpu.make_async_remote_copy(
            src_ref=src.at[:, :, pl.ds(0, n)],
            dst_ref=dst(slot).at[:, :, pl.ds(start, n)],
            send_sem=ext_send.at[0, c], recv_sem=ext_recv.at[slot, c],
            device_id=to_east, device_id_type=MESH,
        )

    def send_chunk(c):
        own_copy(c).start()
        partner_copy(c).start()
        for copy in ext_copies(c):
            copy.start()

    def wait_chunk(slot, c):
        @pl.when(h == slot)
        def _():
            own_copy(c).wait()

        @pl.when(h != slot)
        def _():
            partner_arrival(c).wait_recv()

        if views(c)[2]:
            ext_arrival(slot, c).wait_recv()

    cp_copy = pltpu.make_async_remote_copy(
        src_ref=cp.at[h], dst_ref=cp.at[h],
        send_sem=part_send.at[5], recv_sem=part_recv.at[5],
        device_id=partner, device_id_type=MESH,
    )

    cp_arrival = pltpu.make_async_remote_copy(
        src_ref=cp.at[o], dst_ref=cp.at[o],
        send_sem=part_send.at[5], recv_sem=part_recv.at[5],
        device_id=partner, device_id_type=MESH,
    )

    zero8 = jnp.zeros((F, 2, 8, 128), jnp.float32)
    for slot in range(2):
        for c in (1, 2):
            fr[slot, c, :, :, pl.ds(pl.multiple_of((FRAME - 8) * h, 8), 8)] = zero8
        start = pl.multiple_of(80 * h, 16)
        fr[slot, 0, :, :, pl.ds(start, 16)] = jnp.zeros((F, 2, 16, 128), jnp.float32)

    for i in range(5):
        loads[i].wait()
    for i in range(4):
        for p in range(2):
            tr_o[i, p] = jnp.transpose(nat_o[i, pl.ds(p, 128, stride=2), :])
    pl.semaphore_wait(barrier, count)
    cp_copy.start()
    send_chunk(STEPS)
    for k in (3, 2, 1, 0):
        loads[5 + k].wait()

        def one(f, carry, k=k):
            even_odd[...] = OMEGA * nat_f[k, f].astype(jnp.float32)
            for p in range(2):
                tr_f[k, f, p] = jnp.transpose(even_odd[pl.ds(p, 128, stride=2), :])
            return carry

        lax.fori_loop(0, F, one, 0)
        send_chunk(k)

    lane = lax.broadcasted_iota(jnp.int32, (8, 128), 1)

    def coefficients(slot):
        @pl.when(h == slot)
        def _():
            cp_copy.wait_send()

        @pl.when(h != slot)
        def _():
            cp_arrival.wait_recv()

        table = cp[slot]
        for g in range(F):
            for f in range(F):
                value = jnp.broadcast_to(table[g:g + 1, f:f + 1], (8, 128))
                mix[g, f] = OMEGA * (value + 1.0) if g == f else OMEGA * value

        def one(t, carry):
            def get(i, p, d=0):
                return op[slot, i, p, pl.ds(BASE + t + d, 8, stride=T), :]

            b0, b1 = OMEGA * get(1, 0), OMEGA * get(1, 1)
            v0, v1 = 0.5 * OMEGA * get(3, 0), 0.5 * OMEGA * get(3, 1)
            north = (b0, jnp.where(lane == 127, 0.0, b1))
            south = (jnp.where(lane == 0, 0.0, pltpu.roll(b1, 1, 1)), b0)
            v_north = (v1, jnp.where(lane == 127, 0.0, pltpu.roll(v0, 127, 1)))
            v_south = (jnp.where(lane == 0, 0.0, -pltpu.roll(v1, 1, 1)), -v0)
            for p in range(2):
                east, west = OMEGA * get(0, p), OMEGA * get(0, p, -1)
                co[t, p, 0] = (1.0 - OMEGA) - (east + west + north[p] + south[p])
                co[t, p, 1] = east
                co[t, p, 2] = west
                co[t, p, 3] = north[p]
                co[t, p, 4] = south[p]
                co[t, p, 5] = 0.5 * OMEGA * get(2, p, 1)
                co[t, p, 6] = -0.5 * OMEGA * get(2, p, -1)
                co[t, p, 7] = v_north[p]
                co[t, p, 8] = v_south[p]
            return carry

        lax.fori_loop(0, T, one, 0)

    def pads(buf):
        for p in range(2):
            buf[0, p] = pltpu.roll(buf[T, p], 1, 1)
            buf[T + 1, p] = pltpu.roll(buf[1, p], 7, 1)

    def meridional(here):
        return (here[1], pltpu.roll(here[1], 1, 2)), (pltpu.roll(here[0], 127, 2), here[0])

    def sweep(src, dst, add):
        def one(t, carry):
            here = (src[t + 1, 0], src[t + 1, 1])
            beside = meridional(here)
            for p in range(2):
                diag = co[t, p, 0]
                if add is None:
                    value = (diag + 1.0) * here[p]
                else:
                    value = diag * here[p] + add[t + 1, p]
                value = value + co[t, p, 1] * src[t + 2, p] + co[t, p, 2] * src[t, p]
                value = value + co[t, p, 3] * beside[p][0] + co[t, p, 4] * beside[p][1]
                dst[t + 1, p] = value
            return carry

        lax.fori_loop(0, T, one, 0, unroll=True)
        pads(dst)

    def explicit(slot, k):
        def one(t, carry):
            here = (x2[t + 1, 0], x2[t + 1, 1])
            beside = meridional(here)
            for p in range(2):
                value = fr[slot, k, :, p, strided(t), :]
                value = value + co[t, p, 5] * x2[t + 2, p] + co[t, p, 6] * x2[t, p]
                value = value + co[t, p, 7] * beside[p][0] + co[t, p, 8] * beside[p][1]
                for g in range(F):
                    value = value + mix[g] * here[p][g]
                r[t + 1, p] = value
            return carry

        lax.fori_loop(0, T, one, 0, unroll=True)
        pads(r)

    def wait_forcing(slot, k):
        for c in range(STEPS):
            @pl.when(k == c)
            def _(c=c):
                wait_chunk(slot, c)

    def steps(slot, first):
        def one(n, carry):
            k = STEPS - 1 - n
            sweep(r, x1, None)
            sweep(x1, x2, r)
            wait_forcing(slot, k)
            explicit(slot, k)
            return carry

        lax.fori_loop(first, STEPS, one, 0)

    def from_frame(ref):
        for t in range(T):
            for p in range(2):
                r[t + 1, p] = ref[:, p, strided(t), :]
        pads(r)

    def to_frame(ref):
        for t in range(T):
            for p in range(2):
                ref[:, p, strided(t), :] = r[t + 1, p]

    def edge_copies(target_pair, out_ref, in_ref, send, recv):
        west = (2 * target_pair + o, at_space(-o))
        east = (2 * target_pair + o, at_space(h))
        return [
            pltpu.make_async_remote_copy(
                src_ref=out_ref.at[:, :, pl.ds(HALO, HALO)],
                dst_ref=in_ref.at[:, :, pl.ds(HALO + HALF, HALO)],
                send_sem=send.at[0], recv_sem=recv.at[1],
                device_id=west, device_id_type=MESH,
            ),
            pltpu.make_async_remote_copy(
                src_ref=out_ref.at[:, :, pl.ds(HALF, HALO)],
                dst_ref=in_ref.at[:, :, pl.ds(0, HALO)],
                send_sem=send.at[1], recv_sem=recv.at[0],
                device_id=east, device_id_type=MESH,
            ),
        ]

    def hand_main():
        return pltpu.make_async_remote_copy(
            src_ref=hand_out.at[:, :, pl.ds(HALO, HALF)],
            dst_ref=hand_in.at[:, :, pl.ds(HALO, HALF)],
            send_sem=hand_send.at[2], recv_sem=hand_recv.at[2],
            device_id=(h, space), device_id_type=MESH,
        )

    def result_copy(phase):
        return pltpu.make_async_remote_copy(
            src_ref=adj.at[phase, :, :, pl.ds(HALO, HALF)],
            dst_ref=res.at[:, :, pl.ds(pl.multiple_of(HALF * h, HALF), HALF)],
            send_sem=res_sem.at[0], recv_sem=res_sem.at[1],
            device_id=partner, device_id_type=MESH,
        )

    result_arrival = pltpu.make_async_remote_copy(
        src_ref=adj.at[0, :, :, pl.ds(HALO, HALF)],
        dst_ref=res.at[:, :, pl.ds(pl.multiple_of(HALF * o, HALF), HALF)],
        send_sem=res_sem.at[0], recv_sem=res_sem.at[1],
        device_id=partner, device_id_type=MESH,
    )

    first = pair
    wait_chunk(1, STEPS)
    coefficients(1)

    @pl.when(pair == 1)
    def _():
        wait_chunk(1, 3)
        from_frame(fr.at[1, 3])

    @pl.when(pair == 0)
    def _():
        hand_main().wait_recv()
        for copy in edge_copies(0, hand_out, hand_in, hand_send, hand_recv):
            copy.wait_recv()
        adj[0] = hand_in[...].astype(jnp.float32)
        from_frame(adj.at[0])

    steps(1, first)
    to_frame(adj.at[0])
    edge_out[:, :, HALO:2 * HALO] = adj[0, :, :, HALO:2 * HALO].astype(jnp.bfloat16)
    edge_out[:, :, HALF:HALF + HALO] = adj[0, :, :, HALF:HALF + HALO].astype(jnp.bfloat16)
    edges = edge_copies(pair, edge_out, edge_in, edge_send, edge_recv)
    for copy in edges:
        copy.start()

    @pl.when(h == 0)
    def _():
        result_copy(0).start()

    wait_chunk(0, STEPS)
    coefficients(0)
    for copy in edges:
        copy.wait_recv()
    adj[0, :, :, 0:HALO] = edge_in[:, :, 0:HALO].astype(jnp.float32)
    adj[0, :, :, HALO + HALF:FRAME] = edge_in[:, :, HALO + HALF:FRAME].astype(jnp.float32)
    from_frame(adj.at[0])
    steps(0, 0)
    to_frame(adj.at[1])

    @pl.when(pair == 1)
    def _():
        hand_out[:, :, HALO:HALO + HALF] = adj[1, :, :, HALO:HALO + HALF].astype(jnp.bfloat16)
        hand_main().start()
        for copy in edge_copies(0, hand_out, hand_in, hand_send, hand_recv):
            copy.start()

    @pl.when(h == 1)
    def _():
        result_copy(1).start()

    own = adj.at[1 - h]
    res[:, :, pl.ds(pl.multiple_of(HALF * h, HALF), HALF)] = own[:, :, HALO:HALO + HALF]
    result_arrival.wait_recv()

    def out_copy(f):
        return pltpu.make_async_copy(outv.at[f], out.at[0, f], out_sem.at[f])

    def finish(f, carry):
        for p in range(2):
            outv[f, pl.ds(p, 128, stride=2), :] = (1.0 / OMEGA) * jnp.transpose(res[f, p])
        out_copy(f).start()
        return carry

    lax.fori_loop(0, F, finish, 0)

    for c in range(STEPS + 1):
        partner_copy(c).wait_send()
        for copy in ext_copies(c):
            copy.wait_send()

    for copy in edges:
        copy.wait_send()
    result_copy(0).wait_send()

    @pl.when(pair == 1)
    def _():
        hand_main().wait_send()
        for copy in edge_copies(0, hand_out, hand_in, hand_send, hand_recv):
            copy.wait_send()

    for f in range(F):
        out_copy(f).wait()


def per_device(forcing, zonal_courant, meridional_courant, zonal_faces, meridional_faces, coupling):
    f32, bf16 = jnp.float32, jnp.bfloat16
    dma = pltpu.SemaphoreType.DMA
    return pl.pallas_call(
        body,
        out_shape=jax.ShapeDtypeStruct((1,) + forcing.shape[2:], f32),
        in_specs=[pl.BlockSpec(memory_space=pl.ANY)] * 6,
        out_specs=pl.BlockSpec(memory_space=pl.ANY),
        scratch_shapes=[
            pltpu.VMEM((STEPS, F, 256, 128), bf16),
            pltpu.VMEM((4, 256, 128), f32),
            pltpu.VMEM((256, 128), f32),
            pltpu.VMEM((STEPS, F, 2, 128, 128), f32),
            pltpu.VMEM((4, 2, 128, 128), f32),
            pltpu.VMEM((2, STEPS, F, 2, FRAME, 128), f32),
            pltpu.VMEM((2, 4, 2, FRAME, 128), f32),
            pltpu.VMEM((2, F, F), f32),
            pltpu.VMEM((T, 2, 9, 8, 128), f32),
            pltpu.VMEM((F, F, 8, 128), f32),
            pltpu.VMEM((T + 2, 2, F, 8, 128), f32),
            pltpu.VMEM((T + 2, 2, F, 8, 128), f32),
            pltpu.VMEM((T + 2, 2, F, 8, 128), f32),
            pltpu.VMEM((2, F, 2, FRAME, 128), f32),
            pltpu.VMEM((F, 2, FRAME, 128), bf16),
            pltpu.VMEM((F, 2, FRAME, 128), bf16),
            pltpu.VMEM((F, 2, FRAME, 128), bf16),
            pltpu.VMEM((F, 2, FRAME, 128), bf16),
            pltpu.VMEM((F, 2, 128, 128), f32),
            pltpu.VMEM((F, 256, 128), f32),
            dma((9,)),
            dma((F,)),
            dma((5,)),
            dma((6,)),
            dma((6,)),
            dma((2, 5)),
            dma((2, 5)),
            dma((2,)),
            dma((2,)),
            dma((3,)),
            dma((3,)),
            dma((2,)),
        ],
        compiler_params=pltpu.CompilerParams(
            collective_id=0, has_side_effects=True, vmem_limit_bytes=60 * 1024 * 1024
        ),
        name="adjoint_window",
    )(forcing, zonal_courant, meridional_courant, zonal_faces, meridional_faces, coupling)


def solution(mesh):
    return jax.shard_map(
        per_device,
        mesh=mesh,
        in_specs=(
            P("tm", None, None, None, "space"),
            P("tm", None, "space"),
            P("tm", None, "space"),
            P("tm", None, "space"),
            P("tm", None, "space"),
            P("tm", None, None),
        ),
        out_specs=P("tm", None, None, "space"),
        check_vma=False,
    )
```

time: 688 us -> 52.6 us (0.08)
  the two profiles are of different devices: /device:TPU:2 before, /device:TPU:0 now
where the time goes in v1:
time: 52.6 us; the launch traced here: 52.5 us
  Pallas kernels  49.1 us (93%)
  local copies, waits for them, and re-layouts  3.34 us (6%)
    pallas_call x1, Pallas kernels, per_device(): pl.pallas_call(body, out_shape=jax.ShapeDtypeStruct((1,) + forcing.shape[...  49.1 us
    unnamed x2, local copies, waits for them, and re-layouts  3.34 us

profile of v1, /device:TPU:0, one launch (start us, length us, event | category | flops | bytes accessed | tf_op | source)
XLA Modules:
  0.0 52.5 jit_solution(518222871092910336)
XLA Ops:
  0.0 1.3 %copy.7.coupling = f32[1,6,6]{2,1,0:T(8,128)} copy(f32[1,6,6]{2,0,1:T(1,128)} %param.11) | data formatting | bytes 288 | tf_op args[5]
  1.3 49.1 %adjoint_window.1 = f32[1,6,256,128]{3,2,1,0:T(8,128)} custom-call(bf16[1,4,6,256,128]{4,3,2,1,0:T(8,128)(2,1)} %forcing.1, f32[1,256,128]{2,1,0:T(8,128)} %courant_x.1, f32[1,256,128]{2,1,0:T(8,128)} %courant_y.1, f32[1,256,128]{2,1,0:T(8,128)} %faces_x.1, f32[1,256,128]{2,1,0:T(8,128)} %faces_y.1, f32[1,6,6]{2,1,0:T(8,128)} %copy.7.coupling), custom_call_target="tpu_custom_call" | custom-call | tf_op jit(solution)/shard_map/adjoint_window/pallas_call | solution.py:420
  50.4 2.1 %copy.9 = f32[1,6,256,128]{3,2,1,0:T(8,128)} copy(f32[1,6,256,128]{3,2,1,0:T(8,128)} %adjoint_window.1) | data formatting | bytes 1572864

commit v2 on v1

v2 whole, which is shorter than its diff:
```python
import jax
import jax.numpy as jnp
from jax import lax
from jax.experimental import pallas as pl
from jax.experimental.pallas import tpu as pltpu
from jax.sharding import PartitionSpec as P

OMEGA = 0.4
STEPS = 4
F = 6
WIDTH = 128
HALF = 64
HALO = 24
SIDE = 32
FRAME = HALF + 2 * HALO
T = FRAME // 8
ROWS = WIDTH + 2 * HALO
OPS = STEPS
EXT = ((0, 8, 8, 16, 16), (16, 16, 24, 24, 24))
MESH = pl.DeviceIdType.MESH
UNROLL = True


def body(
    forcing, courant_x, courant_y, faces_x, faces_y, coupling, out,
    nat_f, nat_o, even_odd, fr, op, cp, ops,
    co, mix, r, x1, x2, adj, hand_out, hand_in, side_in, relay_in, res, outv,
    load_sem, out_sem, part_send, part_recv, ext_send, ext_recv,
    hand_send, hand_recv, res_send, res_recv,
):
    tm = lax.axis_index("tm")
    space = lax.axis_index("space")
    n_space = lax.axis_size("space")
    h = lax.rem(tm, 2)
    o = 1 - h
    pair = tm // 2

    def at_space(d):
        return lax.rem(space + d + n_space, n_space)

    barrier = pltpu.get_barrier_semaphore()
    count = 0
    for d in (-1, 1, 0):
        for j in range(4):
            if d == 0 and j == 0:
                continue
            other = lax.rem(tm + j, 4)
            pl.semaphore_signal(barrier, inc=1, device_id=(other, at_space(d)), device_id_type=MESH)
            count += 1

    ops_in = (faces_x, faces_y, courant_x, courant_y)
    loads = [pltpu.make_async_copy(ops_in[i].at[0], nat_o.at[i], load_sem.at[i]) for i in range(4)]
    loads.append(pltpu.make_async_copy(coupling, cp.at[h], load_sem.at[4]))
    loads += [pltpu.make_async_copy(forcing.at[0, k], nat_f.at[k], load_sem.at[5 + k]) for k in range(STEPS)]
    for i in (0, 1, 2, 3, 8, 4, 7, 6, 5):
        loads[i].start()

    partner = (2 * pair + o, space)
    to_east = (2 * pair, at_space(1))
    to_west = (2 * pair + 1, at_space(-1))

    def chunk(slot, c):
        return op.at[slot] if c == OPS else fr.at[slot, c]

    def partner_copy(c):
        ref = chunk(h, c).at[:, :, pl.ds(pl.multiple_of(HALO + 40 * o, 8), 88)]
        return pltpu.make_async_remote_copy(
            src_ref=ref, dst_ref=ref, send_sem=part_send.at[c], recv_sem=part_recv.at[c],
            device_id=partner, device_id_type=MESH,
        )

    def partner_arrival(c):
        ref = chunk(o, c).at[:, :, pl.ds(pl.multiple_of(HALO + 40 * h, 8), 88)]
        return pltpu.make_async_remote_copy(
            src_ref=ref, dst_ref=ref, send_sem=part_send.at[c], recv_sem=part_recv.at[c],
            device_id=partner, device_id_type=MESH,
        )

    def ext_copies(slot, c):
        n = EXT[slot][c]
        if n == 0:
            return []
        ref = chunk(slot, c)
        east = pltpu.make_async_remote_copy(
            src_ref=ref.at[:, :, pl.ds(HALO + WIDTH - n, n)],
            dst_ref=ref.at[:, :, pl.ds(HALO - n, n)],
            send_sem=ext_send.at[0, c], recv_sem=ext_recv.at[slot, c],
            device_id=to_east, device_id_type=MESH,
        )
        west = pltpu.make_async_remote_copy(
            src_ref=ref.at[:, :, pl.ds(HALO, n)],
            dst_ref=ref.at[:, :, pl.ds(HALO + WIDTH, n)],
            send_sem=ext_send.at[1, c], recv_sem=ext_recv.at[slot, c],
            device_id=to_west, device_id_type=MESH,
        )
        return [east, west]

    def ext_arrival(slot, c):
        n = EXT[slot][c]
        start = pl.multiple_of((HALO - n) * o + (HALO + WIDTH) * h, 8)
        ref = chunk(slot, c).at[:, :, pl.ds(start, n)]
        return pltpu.make_async_remote_copy(
            src_ref=ref, dst_ref=ref, send_sem=ext_send.at[0, c], recv_sem=ext_recv.at[slot, c],
            device_id=to_east, device_id_type=MESH,
        )

    def wait_chunk(slot, c):
        @pl.when(h != slot)
        def _():
            partner_arrival(c).wait_recv()

        if EXT[slot][c]:
            ext_arrival(slot, c).wait_recv()

    def cp_copy(slot):
        return pltpu.make_async_remote_copy(
            src_ref=cp.at[slot], dst_ref=cp.at[slot],
            send_sem=part_send.at[5], recv_sem=part_recv.at[5],
            device_id=partner, device_id_type=MESH,
        )

    for slot in range(2):
        for c in range(STEPS + 1):
            n = EXT[slot][c]
            if n < HALO:
                ref = chunk(slot, c)
                start = pl.multiple_of((HALO + WIDTH + n) * h, 8)
                ref[:, :, pl.ds(start, HALO - n)] = jnp.zeros(ref.shape[:2] + (HALO - n, 128), jnp.float32)

    for i in range(4):
        loads[i].wait()
    for i in range(4):
        for p in range(2):
            op[h, i, p, HALO:HALO + WIDTH] = jnp.transpose(nat_o[i, pl.ds(p, 128, stride=2), :])
    pl.semaphore_wait(barrier, count)

    def send_first(c):
        @pl.when(h == 1)
        def _():
            for copy in ext_copies(1, c):
                copy.start()

        partner_copy(c).start()

    send_first(OPS)
    for k in (3, 2, 1, 0):
        loads[5 + k].wait()

        def one(f, carry, k=k):
            even_odd[...] = OMEGA * nat_f[k, f].astype(jnp.float32)
            for p in range(2):
                fr[h, k, f, p, HALO:HALO + WIDTH] = jnp.transpose(even_odd[pl.ds(p, 128, stride=2), :])
            return carry

        lax.fori_loop(0, F, one, 0)
        send_first(k)
        if k == 3:
            loads[4].wait()
            cp_copy(h).start()

    @pl.when(h == 0)
    def _():
        for c in (OPS, 3, 2, 1, 0):
            for copy in ext_copies(0, c):
                copy.start()

    lane = lax.broadcasted_iota(jnp.int32, (8, 128), 1)

    def frame(t):
        return pl.ds(HALF * h + t, 8, stride=T)

    def coefficients(slot):
        @pl.when(h != slot)
        def _():
            cp_copy(o).wait_recv()

        for g in range(F):
            row = cp[slot, g]
            for f in range(F):
                value = jnp.broadcast_to(row[:, f:f + 1], (8, 128))
                mix[g, f] = OMEGA * (value + 1.0) if g == f else OMEGA * value

        for i in (0, 2):
            for p in range(2):
                for t in range(T):
                    ops[i // 2, t + 1, p] = op[slot, i, p, frame(t), :]
                ops[i // 2, 0, p] = pltpu.roll(ops[i // 2, T, p], 1, 0)
                ops[i // 2, T + 1, p] = pltpu.roll(ops[i // 2, 1, p], 7, 0)

        def one(t, carry):
            def get(i, p):
                return op[slot, i, p, frame(t), :]

            b0, b1 = OMEGA * get(1, 0), OMEGA * get(1, 1)
            v0, v1 = 0.5 * OMEGA * get(3, 0), 0.5 * OMEGA * get(3, 1)
            north = (b0, jnp.where(lane == 127, 0.0, b1))
            south = (jnp.where(lane == 0, 0.0, pltpu.roll(b1, 1, 1)), b0)
            v_north = (v1, jnp.where(lane == 127, 0.0, pltpu.roll(v0, 127, 1)))
            v_south = (jnp.where(lane == 0, 0.0, -pltpu.roll(v1, 1, 1)), -v0)
            for p in range(2):
                east, west = OMEGA * ops[0, t + 1, p], OMEGA * ops[0, t, p]
                co[t, p, 0] = (1.0 - OMEGA) - (east + west + north[p] + south[p])
                co[t, p, 1] = east
                co[t, p, 2] = west
                co[t, p, 3] = north[p]
                co[t, p, 4] = south[p]
                co[t, p, 5] = 0.5 * OMEGA * ops[1, t + 2, p]
                co[t, p, 6] = -0.5 * OMEGA * ops[1, t, p]
                co[t, p, 7] = v_north[p]
                co[t, p, 8] = v_south[p]
            return carry

        lax.fori_loop(0, T, one, 0)

    def pads(buf):
        for p in range(2):
            buf[0, p] = pltpu.roll(buf[T, p], 1, 1)
            buf[T + 1, p] = pltpu.roll(buf[1, p], 7, 1)

    def meridional(here):
        return (here[1], pltpu.roll(here[1], 1, 2)), (pltpu.roll(here[0], 127, 2), here[0])

    def sweep(src, dst, add):
        def one(t, carry):
            here = (src[t + 1, 0], src[t + 1, 1])
            beside = meridional(here)
            for p in range(2):
                diag = co[t, p, 0]
                if add is None:
                    value = (diag + 1.0) * here[p]
                else:
                    value = diag * here[p] + add[t + 1, p]
                value = value + co[t, p, 1] * src[t + 2, p] + co[t, p, 2] * src[t, p]
                value = value + co[t, p, 3] * beside[p][0] + co[t, p, 4] * beside[p][1]
                dst[t + 1, p] = value
            return carry

        lax.fori_loop(0, T, one, 0, unroll=UNROLL)
        pads(dst)

    def explicit(slot, k):
        def one(t, carry):
            here = (x2[t + 1, 0], x2[t + 1, 1])
            beside = meridional(here)
            for p in range(2):
                value = fr[slot, k, :, p, frame(t), :]
                value = value + co[t, p, 5] * x2[t + 2, p] + co[t, p, 6] * x2[t, p]
                value = value + co[t, p, 7] * beside[p][0] + co[t, p, 8] * beside[p][1]
                for g in range(F):
                    value = value + mix[g] * here[p][g]
                r[t + 1, p] = value
            return carry

        lax.fori_loop(0, T, one, 0, unroll=UNROLL)
        pads(r)

    def steps(slot, first):
        def one(n, carry):
            k = STEPS - 1 - n
            sweep(r, x1, None)
            sweep(x1, x2, r)
            for c in range(STEPS):
                @pl.when(k == c)
                def _(c=c):
                    wait_chunk(slot, c)

            explicit(slot, k)
            return carry

        lax.fori_loop(first, STEPS, one, 0)

    def adj_frame(t):
        return pl.ds(SIDE - HALO + t, 8, stride=T)

    def to_adj(phase):
        for t in range(T):
            for p in range(2):
                adj[phase, :, p, adj_frame(t), :] = r[t + 1, p]

    def result_copy(phase, f):
        return pltpu.make_async_remote_copy(
            src_ref=adj.at[phase, f, :, pl.ds(SIDE, HALF)],
            dst_ref=res.at[f, :, pl.ds(pl.multiple_of(HALF * h, HALF), HALF)],
            send_sem=res_send.at[f], recv_sem=res_recv.at[f],
            device_id=partner, device_id_type=MESH,
        )

    def result_arrival(f):
        return pltpu.make_async_remote_copy(
            src_ref=adj.at[0, f, :, pl.ds(SIDE, HALF)],
            dst_ref=res.at[f, :, pl.ds(pl.multiple_of(HALF * o, HALF), HALF)],
            send_sem=res_send.at[f], recv_sem=res_recv.at[f],
            device_id=partner, device_id_type=MESH,
        )

    def hand_main():
        return pltpu.make_async_remote_copy(
            src_ref=hand_out, dst_ref=hand_in, send_sem=hand_send.at[0], recv_sem=hand_recv.at[0],
            device_id=(h, space), device_id_type=MESH,
        )

    def hand_side():
        return pltpu.make_async_remote_copy(
            src_ref=hand_out.at[:, :, pl.ds(pl.multiple_of(SIDE * h, SIDE), SIDE)], dst_ref=side_in,
            send_sem=hand_send.at[1], recv_sem=hand_recv.at[1],
            device_id=(o, at_space(2 * h - 1)), device_id_type=MESH,
        )

    def relay():
        return pltpu.make_async_remote_copy(
            src_ref=hand_in.at[:, :, pl.ds(pl.multiple_of(SIDE * o, SIDE), SIDE)], dst_ref=relay_in,
            send_sem=hand_send.at[2], recv_sem=hand_recv.at[2],
            device_id=partner, device_id_type=MESH,
        )

    wait_chunk(1, OPS)
    coefficients(1)

    @pl.when(pair == 1)
    def _():
        wait_chunk(1, 3)
        for t in range(T):
            for p in range(2):
                r[t + 1, p] = fr[1, 3, :, p, frame(t), :]

    @pl.when(pair == 0)
    def _():
        hand_main().wait_recv()
        relay().start()
        adj[0, :, :, SIDE:SIDE + HALF] = hand_in[...].astype(jnp.float32)
        hand_side().wait_recv()
        adj[0, :, :, pl.ds(pl.multiple_of((SIDE + HALF) * h, SIDE), SIDE)] = side_in[...].astype(jnp.float32)
        relay().wait_recv()
        adj[0, :, :, pl.ds(pl.multiple_of((SIDE + HALF) * o, SIDE), SIDE)] = relay_in[...].astype(jnp.float32)
        for t in range(T):
            for p in range(2):
                r[t + 1, p] = adj[0, :, p, adj_frame(t), :]

    pads(r)
    steps(1, pair)
    to_adj(0)

    @pl.when(h == 0)
    def _():
        for f in range(F):
            result_copy(0, f).start()

    wait_chunk(0, OPS)
    coefficients(0)
    steps(0, 0)
    to_adj(1)

    @pl.when(pair == 1)
    def _():
        hand_out[...] = adj[1, :, :, SIDE:SIDE + HALF].astype(jnp.bfloat16)
        hand_side().start()
        hand_main().start()

    @pl.when(h == 1)
    def _():
        for f in range(F):
            result_copy(1, f).start()

    def out_copy(f):
        return pltpu.make_async_copy(outv.at[f], out.at[0, f], out_sem.at[f])

    own = adj.at[1 - h]
    res[:, :, pl.ds(pl.multiple_of(HALF * h, HALF), HALF)] = own[:, :, SIDE:SIDE + HALF]
    for f in range(F):
        result_arrival(f).wait_recv()
        for p in range(2):
            outv[f, pl.ds(p, 128, stride=2), :] = (1.0 / OMEGA) * jnp.transpose(res[f, p])
        out_copy(f).start()

    for c in range(STEPS + 1):
        partner_copy(c).wait_send()
    for slot in range(2):
        @pl.when(h == slot)
        def _(slot=slot):
            for c in range(STEPS + 1):
                for copy in ext_copies(slot, c):
                    copy.wait_send()

    cp_copy(h).wait_send()
    for f in range(F):
        result_copy(0, f).wait_send()

    @pl.when(pair == 1)
    def _():
        hand_main().wait_send()
        hand_side().wait_send()

    @pl.when(pair == 0)
    def _():
        relay().wait_send()

    for f in range(F):
        out_copy(f).wait()


def per_device(forcing, zonal_courant, meridional_courant, zonal_faces, meridional_faces, coupling):
    f32, bf16 = jnp.float32, jnp.bfloat16
    dma = pltpu.SemaphoreType.DMA
    state = pltpu.VMEM((T + 2, 2, F, 8, 128), f32)
    return pl.pallas_call(
        body,
        out_shape=jax.ShapeDtypeStruct((1,) + forcing.shape[2:], f32),
        in_specs=[pl.BlockSpec(memory_space=pl.ANY)] * 6,
        out_specs=pl.BlockSpec(memory_space=pl.ANY),
        scratch_shapes=[
            pltpu.VMEM((STEPS, F, 256, 128), bf16),
            pltpu.VMEM((4, 256, 128), f32),
            pltpu.VMEM((256, 128), f32),
            pltpu.VMEM((2, STEPS, F, 2, ROWS, 128), f32),
            pltpu.VMEM((2, 4, 2, ROWS, 128), f32),
            pltpu.VMEM((2, F, 1, F), f32),
            pltpu.VMEM((2, T + 2, 2, 8, 128), f32),
            pltpu.VMEM((T, 2, 9, 8, 128), f32),
            pltpu.VMEM((F, F, 8, 128), f32),
            state, state, state,
            pltpu.VMEM((2, F, 2, HALF + 2 * SIDE, 128), f32),
            pltpu.VMEM((F, 2, HALF, 128), bf16),
            pltpu.VMEM((F, 2, HALF, 128), bf16),
            pltpu.VMEM((F, 2, SIDE, 128), bf16),
            pltpu.VMEM((F, 2, SIDE, 128), bf16),
            pltpu.VMEM((F, 2, WIDTH, 128), f32),
            pltpu.VMEM((F, 256, 128), f32),
            dma((9,)), dma((F,)),
            dma((6,)), dma((6,)),
            dma((2, 5)), dma((2, 5)),
            dma((3,)), dma((3,)),
            dma((F,)), dma((F,)),
        ],
        compiler_params=pltpu.CompilerParams(
            collective_id=0, has_side_effects=True, vmem_limit_bytes=60 * 1024 * 1024
        ),
        name="adjoint_window",
    )(forcing, zonal_courant, meridional_courant, zonal_faces, meridional_faces, jnp.transpose(coupling, (1, 0, 2)))


def solution(mesh):
    return jax.shard_map(
        per_device,
        mesh=mesh,
        in_specs=(
            P("tm", None, None, None, "space"),
            P("tm", None, "space"),
            P("tm", None, "space"),
            P("tm", None, "space"),
            P("tm", None, "space"),
            P("tm", None, None),
        ),
        out_specs=P("tm", None, None, "space"),
        check_vma=False,
    )
```

time: 52.6 us -> 49.5 us (0.941)
  Pallas kernels: 49.1 us -> 47.3 us
  local copies, waits for them, and re-layouts: 3.34 us -> 2.06 us
    pallas_call x1, Pallas kernels: 49.1 us -> 47.3 us  [per_device(): pl.pallas_call(body, out_shape=jax.ShapeDtypeStruct((1,) + forcing.shape[...]
    unnamed x2 -> x1, local copies, waits for them, and re-layouts: 3.34 us -> 2.06 us
where the time goes in v2:
time: 49.5 us; the launch traced here: 49.4 us
  Pallas kernels  47.3 us (96%)
  local copies, waits for them, and re-layouts  2.06 us (4%)
    pallas_call x1, Pallas kernels, per_device(): pl.pallas_call(body, out_shape=jax.ShapeDtypeStruct((1,) + forcing.shape[...  47.3 us
    unnamed x1, local copies, waits for them, and re-layouts  2.06 us

profile of v2, /device:TPU:0, one launch (start us, length us, event | category | flops | bytes accessed | tf_op | source)
XLA Modules:
  0.0 49.4 jit_solution(17408425556802448052)
XLA Ops:
  0.0 47.3 %adjoint_window.1 = f32[1,6,256,128]{3,2,1,0:T(8,128)} custom-call(bf16[1,4,6,256,128]{4,3,2,1,0:T(8,128)(2,1)} %forcing.1, f32[1,256,128]{2,1,0:T(8,128)} %courant_x.1, f32[1,256,128]{2,1,0:T(8,128)} %courant_y.1, f32[1,256,128]{2,1,0:T(8,128)} %faces_x.1, f32[1,256,128]{2,1,0:T(8,128)} %faces_y.1, f32[6,1,6]{2,1,0:T(1,128)} %bitcast.1), custom_call_target="tpu_custom_call" | custom-call | tf_op jit(solution)/shard_map/adjoint_window/pallas_call | solution.py:405
  47.3 2.1 %copy.8 = f32[1,6,256,128]{3,2,1,0:T(8,128)} copy(f32[1,6,256,128]{3,2,1,0:T(8,128)} %adjoint_window.1) | data formatting | bytes 1572864

commit v3 on v2

--- a/solution.py
+++ b/solution.py
@@ -12,8 +12,9 @@
 HALF = 64
 HALO = 24
 SIDE = 32
-FRAME = HALF + 2 * HALO
-T = FRAME // 8
+TS = (11, 14)
+T = max(TS)
+WEST = (12, 24)
 ROWS = WIDTH + 2 * HALO
 OPS = STEPS
 EXT = ((0, 8, 8, 16, 16), (16, 16, 24, 24, 24))
@@ -23,8 +24,8 @@
 
 def body(
     forcing, courant_x, courant_y, faces_x, faces_y, coupling, out,
-    nat_f, nat_o, even_odd, fr, op, cp, ops,
-    co, mix, r, x1, x2, adj, hand_out, hand_in, side_in, relay_in, res, outv,
+    nat_f, nat_o, even_odd, fr, op, cp, ops, ext_out, ext_in,
+    co, mix, r, x1, x2, r_n, x1_n, x2_n, adj, hand_out, hand_in, side_in, relay_in, res, outv,
     load_sem, out_sem, part_send, part_recv, ext_send, ext_recv,
     hand_send, hand_recv, res_send, res_recv,
 ):
@@ -76,33 +77,50 @@
             device_id=partner, device_id_type=MESH,
         )
 
+    def ext_ends(slot, c, side):
+        n = EXT[slot][c]
+        if c == OPS:
+            start = (HALO + WIDTH - n, HALO)[side]
+            there = (HALO - n, HALO + WIDTH)[side]
+            return op.at[slot, :, :, pl.ds(start, n)], op.at[slot, :, :, pl.ds(there, n)]
+        return ext_out.at[side, c, :, pl.ds(0, 2 * n)], ext_in.at[slot, c, :, pl.ds(0, 2 * n)]
+
+    def ext_pack(slot, c):
+        n = EXT[slot][c]
+        if c < OPS and n:
+            for side in range(2):
+                start = (HALO + WIDTH - n, HALO)[side]
+                both = jnp.concatenate([fr[slot, c, :, p, start:start + n] for p in range(2)], axis=1)
+                ext_out[side, c, :, 0:2 * n] = both.astype(jnp.bfloat16)
+
     def ext_copies(slot, c):
-        n = EXT[slot][c]
-        if n == 0:
+        if EXT[slot][c] == 0:
             return []
-        ref = chunk(slot, c)
-        east = pltpu.make_async_remote_copy(
-            src_ref=ref.at[:, :, pl.ds(HALO + WIDTH - n, n)],
-            dst_ref=ref.at[:, :, pl.ds(HALO - n, n)],
-            send_sem=ext_send.at[0, c], recv_sem=ext_recv.at[slot, c],
-            device_id=to_east, device_id_type=MESH,
-        )
-        west = pltpu.make_async_remote_copy(
-            src_ref=ref.at[:, :, pl.ds(HALO, n)],
-            dst_ref=ref.at[:, :, pl.ds(HALO + WIDTH, n)],
-            send_sem=ext_send.at[1, c], recv_sem=ext_recv.at[slot, c],
-            device_id=to_west, device_id_type=MESH,
-        )
-        return [east, west]
+        copies = []
+        for side in range(2):
+            src, dst = ext_ends(slot, c, side)
+            copies.append(pltpu.make_async_remote_copy(
+                src_ref=src, dst_ref=dst,
+                send_sem=ext_send.at[side, c], recv_sem=ext_recv.at[slot, c],
+                device_id=(to_east, to_west)[side], device_id_type=MESH,
+            ))
+        return copies
 
     def ext_arrival(slot, c):
         n = EXT[slot][c]
         start = pl.multiple_of((HALO - n) * o + (HALO + WIDTH) * h, 8)
-        ref = chunk(slot, c).at[:, :, pl.ds(start, n)]
-        return pltpu.make_async_remote_copy(
+        if c == OPS:
+            ref = op.at[slot, :, :, pl.ds(start, n)]
+        else:
+            ref = ext_in.at[slot, c, :, pl.ds(0, 2 * n)]
+        pltpu.make_async_remote_copy(
             src_ref=ref, dst_ref=ref, send_sem=ext_send.at[0, c], recv_sem=ext_recv.at[slot, c],
             device_id=to_east, device_id_type=MESH,
-        )
+        ).wait_recv()
+        if c < OPS:
+            both = ext_in[slot, c, :, 0:2 * n].astype(jnp.float32)
+            for p in range(2):
+                fr[slot, c, :, p, pl.ds(start, n)] = both[:, p * n:(p + 1) * n]
 
     def wait_chunk(slot, c):
         @pl.when(h != slot)
@@ -110,7 +128,7 @@
             partner_arrival(c).wait_recv()
 
         if EXT[slot][c]:
-            ext_arrival(slot, c).wait_recv()
+            ext_arrival(slot, c)
 
     def cp_copy(slot):
         return pltpu.make_async_remote_copy(
@@ -137,6 +155,7 @@
     def send_first(c):
         @pl.when(h == 1)
         def _():
+            ext_pack(1, c)
             for copy in ext_copies(1, c):
                 copy.start()
 
@@ -147,7 +166,7 @@
         loads[5 + k].wait()
 
         def one(f, carry, k=k):
-            even_odd[...] = OMEGA * nat_f[k, f].astype(jnp.float32)
+            even_odd[...] = nat_f[k, f].astype(jnp.float32)
             for p in range(2):
                 fr[h, k, f, p, HALO:HALO + WIDTH] = jnp.transpose(even_odd[pl.ds(p, 128, stride=2), :])
             return carry
@@ -161,35 +180,37 @@
     @pl.when(h == 0)
     def _():
         for c in (OPS, 3, 2, 1, 0):
+            ext_pack(0, c)
             for copy in ext_copies(0, c):
                 copy.start()
 
     lane = lax.broadcasted_iota(jnp.int32, (8, 128), 1)
 
-    def frame(t):
-        return pl.ds(HALF * h + t, 8, stride=T)
+    def frame(slot, t):
+        return pl.ds(HALF * h + HALO - WEST[slot] + t, 8, stride=TS[slot])
 
     def coefficients(slot):
         @pl.when(h != slot)
         def _():
             cp_copy(o).wait_recv()
 
+        last = TS[slot]
         for g in range(F):
             row = cp[slot, g]
             for f in range(F):
                 value = jnp.broadcast_to(row[:, f:f + 1], (8, 128))
-                mix[g, f] = OMEGA * (value + 1.0) if g == f else OMEGA * value
+                mix[slot, g, f] = OMEGA * (value + 1.0) if g == f else OMEGA * value
 
         for i in (0, 2):
             for p in range(2):
-                for t in range(T):
-                    ops[i // 2, t + 1, p] = op[slot, i, p, frame(t), :]
-                ops[i // 2, 0, p] = pltpu.roll(ops[i // 2, T, p], 1, 0)
-                ops[i // 2, T + 1, p] = pltpu.roll(ops[i // 2, 1, p], 7, 0)
+                for t in range(last):
+                    ops[i // 2, t + 1, p] = op[slot, i, p, frame(slot, t), :]
+                ops[i // 2, 0, p] = pltpu.roll(ops[i // 2, last, p], 1, 0)
+                ops[i // 2, last + 1, p] = pltpu.roll(ops[i // 2, 1, p], 7, 0)
 
         def one(t, carry):
             def get(i, p):
-                return op[slot, i, p, frame(t), :]
+                return op[slot, i, p, frame(slot, t), :]
 
             b0, b1 = OMEGA * get(1, 0), OMEGA * get(1, 1)
             v0, v1 = 0.5 * OMEGA * get(3, 0), 0.5 * OMEGA * get(3, 1)
@@ -199,68 +220,65 @@
             v_south = (jnp.where(lane == 0, 0.0, -pltpu.roll(v1, 1, 1)), -v0)
             for p in range(2):
                 east, west = OMEGA * ops[0, t + 1, p], OMEGA * ops[0, t, p]
-                co[t, p, 0] = (1.0 - OMEGA) - (east + west + north[p] + south[p])
-                co[t, p, 1] = east
-                co[t, p, 2] = west
-                co[t, p, 3] = north[p]
-                co[t, p, 4] = south[p]
-                co[t, p, 5] = 0.5 * OMEGA * ops[1, t + 2, p]
-                co[t, p, 6] = -0.5 * OMEGA * ops[1, t, p]
-                co[t, p, 7] = v_north[p]
-                co[t, p, 8] = v_south[p]
+                co[slot, t, p, 0] = (1.0 - OMEGA) - (east + west + north[p] + south[p])
+                co[slot, t, p, 1] = east
+                co[slot, t, p, 2] = west
+                co[slot, t, p, 3] = (south, north)[p][p]
+                co[slot, t, p, 4] = (north, south)[p][p]
+                co[slot, t, p, 5] = 0.5 * OMEGA * ops[1, t + 2, p]
+                co[slot, t, p, 6] = -0.5 * OMEGA * ops[1, t, p]
+                co[slot, t, p, 7] = (v_south, v_north)[p][p]
+                co[slot, t, p, 8] = (v_north, v_south)[p][p]
             return carry
 
-        lax.fori_loop(0, T, one, 0)
-
-    def pads(buf):
+        lax.fori_loop(0, last, one, 0)
+
+    def pads(slot, buf):
         for p in range(2):
-            buf[0, p] = pltpu.roll(buf[T, p], 1, 1)
-            buf[T + 1, p] = pltpu.roll(buf[1, p], 7, 1)
-
-    def meridional(here):
-        return (here[1], pltpu.roll(here[1], 1, 2)), (pltpu.roll(here[0], 127, 2), here[0])
-
-    def sweep(src, dst, add):
+            buf[0, p] = pltpu.roll(buf[TS[slot], p], 1, 1)
+            buf[TS[slot] + 1, p] = pltpu.roll(buf[1, p], 7, 1)
+
+    def store(dst, dst_n, t, p, value):
+        dst[t + 1, p] = value
+        dst_n[t + 1, 1 - p] = pltpu.roll(value, 1 if p else 127, 2)
+
+    def sweep(slot, src, src_n, dst, dst_n, add):
         def one(t, carry):
-            here = (src[t + 1, 0], src[t + 1, 1])
-            beside = meridional(here)
-            for p in range(2):
-                diag = co[t, p, 0]
+            for p in range(2):
+                diag = co[slot, t, p, 0]
                 if add is None:
-                    value = (diag + 1.0) * here[p]
+                    value = (diag + 1.0) * src[t + 1, p]
                 else:
-                    value = diag * here[p] + add[t + 1, p]
-                value = value + co[t, p, 1] * src[t + 2, p] + co[t, p, 2] * src[t, p]
-                value = value + co[t, p, 3] * beside[p][0] + co[t, p, 4] * beside[p][1]
-                dst[t + 1, p] = value
+                    value = diag * src[t + 1, p] + add[t + 1, p]
+                value = value + co[slot, t, p, 1] * src[t + 2, p] + co[slot, t, p, 2] * src[t, p]
+                value = value + co[slot, t, p, 3] * src_n[t + 1, p] + co[slot, t, p, 4] * src[t + 1, 1 - p]
+                store(dst, dst_n, t, p, value)
             return carry
 
-        lax.fori_loop(0, T, one, 0, unroll=UNROLL)
-        pads(dst)
+        lax.fori_loop(0, TS[slot], one, 0, unroll=UNROLL)
+        pads(slot, dst)
 
     def explicit(slot, k):
         def one(t, carry):
-            here = (x2[t + 1, 0], x2[t + 1, 1])
-            beside = meridional(here)
-            for p in range(2):
-                value = fr[slot, k, :, p, frame(t), :]
-                value = value + co[t, p, 5] * x2[t + 2, p] + co[t, p, 6] * x2[t, p]
-                value = value + co[t, p, 7] * beside[p][0] + co[t, p, 8] * beside[p][1]
+            for p in range(2):
+                value = fr[slot, k, :, p, frame(slot, t), :]
+                value = value + co[slot, t, p, 5] * x2[t + 2, p] + co[slot, t, p, 6] * x2[t, p]
+                value = value + co[slot, t, p, 7] * x2_n[t + 1, p] + co[slot, t, p, 8] * x2[t + 1, 1 - p]
                 for g in range(F):
-                    value = value + mix[g] * here[p][g]
-                r[t + 1, p] = value
+                    value = value + mix[slot, g] * x2[t + 1, p, g]
+                store(r, r_n, t, p, value)
             return carry
 
-        lax.fori_loop(0, T, one, 0, unroll=UNROLL)
-        pads(r)
+        lax.fori_loop(0, TS[slot], one, 0, unroll=UNROLL)
+        pads(slot, r)
 
     def steps(slot, first):
         def one(n, carry):
             k = STEPS - 1 - n
-            sweep(r, x1, None)
-            sweep(x1, x2, r)
+            sweep(slot, r, r_n, x1, x1_n, None)
+            sweep(slot, x1, x1_n, x2, x2_n, r)
             for c in range(STEPS):
-                @pl.when(k == c)
+                @pl.when((k == c) & (pair == 1))
                 def _(c=c):
                     wait_chunk(slot, c)
 
@@ -269,13 +287,19 @@
 
         lax.fori_loop(first, STEPS, one, 0)
 
-    def adj_frame(t):
-        return pl.ds(SIDE - HALO + t, 8, stride=T)
-
-    def to_adj(phase):
-        for t in range(T):
-            for p in range(2):
-                adj[phase, :, p, adj_frame(t), :] = r[t + 1, p]
+    def adj_frame(slot, t):
+        return pl.ds(SIDE - WEST[slot] + t, 8, stride=TS[slot])
+
+    def to_adj(slot):
+        for t in range(TS[slot]):
+            for p in range(2):
+                adj[1 - slot, :, p, adj_frame(slot, t), :] = r[t + 1, p]
+
+    def from_adj(slot):
+        for t in range(TS[slot]):
+            for p in range(2):
+                store(r, r_n, t, p, adj[0, :, p, adj_frame(slot, t), :])
+        pads(slot, r)
 
     def result_copy(phase, f):
         return pltpu.make_async_remote_copy(
@@ -319,12 +343,18 @@
     @pl.when(pair == 1)
     def _():
         wait_chunk(1, 3)
-        for t in range(T):
-            for p in range(2):
-                r[t + 1, p] = fr[1, 3, :, p, frame(t), :]
+        for t in range(TS[1]):
+            for p in range(2):
+                store(r, r_n, t, p, fr[1, 3, :, p, frame(1, t), :])
+        pads(1, r)
 
     @pl.when(pair == 0)
     def _():
+        wait_chunk(0, OPS)
+        coefficients(0)
+        for slot in (1, 0):
+            for c in range(STEPS):
+                wait_chunk(slot, c)
         hand_main().wait_recv()
         relay().start()
         adj[0, :, :, SIDE:SIDE + HALF] = hand_in[...].astype(jnp.float32)
@@ -332,23 +362,24 @@
         adj[0, :, :, pl.ds(pl.multiple_of((SIDE + HALF) * h, SIDE), SIDE)] = side_in[...].astype(jnp.float32)
         relay().wait_recv()
         adj[0, :, :, pl.ds(pl.multiple_of((SIDE + HALF) * o, SIDE), SIDE)] = relay_in[...].astype(jnp.float32)
-        for t in range(T):
-            for p in range(2):
-                r[t + 1, p] = adj[0, :, p, adj_frame(t), :]
-
-    pads(r)
+        from_adj(1)
+
     steps(1, pair)
-    to_adj(0)
+    to_adj(1)
 
     @pl.when(h == 0)
     def _():
         for f in range(F):
             result_copy(0, f).start()
 
-    wait_chunk(0, OPS)
-    coefficients(0)
+    @pl.when(pair == 1)
+    def _():
+        wait_chunk(0, OPS)
+        coefficients(0)
+
+    from_adj(0)
     steps(0, 0)
-    to_adj(1)
+    to_adj(0)
 
     @pl.when(pair == 1)
     def _():
@@ -369,7 +400,7 @@
     for f in range(F):
         result_arrival(f).wait_recv()
         for p in range(2):
-            outv[f, pl.ds(p, 128, stride=2), :] = (1.0 / OMEGA) * jnp.transpose(res[f, p])
+            outv[f, pl.ds(p, 128, stride=2), :] = jnp.transpose(res[f, p])
         out_copy(f).start()
 
     for c in range(STEPS + 1):
@@ -402,6 +433,7 @@
     f32, bf16 = jnp.float32, jnp.bfloat16
     dma = pltpu.SemaphoreType.DMA
     state = pltpu.VMEM((T + 2, 2, F, 8, 128), f32)
+    beside = pltpu.VMEM((T + 1, 2, F, 8, 128), f32)
     return pl.pallas_call(
         body,
         out_shape=jax.ShapeDtypeStruct((1,) + forcing.shape[2:], f32),
@@ -415,9 +447,11 @@
             pltpu.VMEM((2, 4, 2, ROWS, 128), f32),
             pltpu.VMEM((2, F, 1, F), f32),
             pltpu.VMEM((2, T + 2, 2, 8, 128), f32),
-            pltpu.VMEM((T, 2, 9, 8, 128), f32),
-            pltpu.VMEM((F, F, 8, 128), f32),
-            state, state, state,
+            pltpu.VMEM((2, STEPS, F, 2 * HALO, 128), bf16),
+            pltpu.VMEM((2, STEPS, F, 2 * HALO, 128), bf16),
+            pltpu.VMEM((2, T, 2, 9, 8, 128), f32),
+            pltpu.VMEM((2, F, F, 8, 128), f32),
+            state, state, state, beside, beside, beside,
             pltpu.VMEM((2, F, 2, HALF + 2 * SIDE, 128), f32),
             pltpu.VMEM((F, 2, HALF, 128), bf16),
             pltpu.VMEM((F, 2, HALF, 128), bf16),

time: 49.5 us -> 43.2 us (0.87)
  Pallas kernels: 47.3 us -> 40.7 us
    pallas_call x1, Pallas kernels: 47.3 us -> 40.7 us  [per_device(): pl.pallas_call(body, out_shape=jax.ShapeDtypeStruct((1,) + forcing.shape[...]
where the time goes in v3:
time: 43.2 us; the launch traced here: 42.8 us
  Pallas kernels  40.7 us (94%)
  local copies, waits for them, and re-layouts  2.06 us (5%)
    pallas_call x1, Pallas kernels, per_device(): pl.pallas_call(body, out_shape=jax.ShapeDtypeStruct((1,) + forcing.shape[...  40.7 us
    unnamed x1, local copies, waits for them, and re-layouts  2.06 us

profile of v3, /device:TPU:0, one launch (start us, length us, event | category | flops | bytes accessed | tf_op | source)
XLA Modules:
  0.0 42.8 jit_solution(2977803603597057108)
XLA Ops:
  0.0 40.7 %adjoint_window.1 = f32[1,6,256,128]{3,2,1,0:T(8,128)} custom-call(bf16[1,4,6,256,128]{4,3,2,1,0:T(8,128)(2,1)} %forcing.1, f32[1,256,128]{2,1,0:T(8,128)} %courant_x.1, f32[1,256,128]{2,1,0:T(8,128)} %courant_y.1, f32[1,256,128]{2,1,0:T(8,128)} %faces_x.1, f32[1,256,128]{2,1,0:T(8,128)} %faces_y.1, f32[6,1,6]{2,1,0:T(1,128)} %bitcast.1), custom_call_target="tpu_custom_call" | custom-call | tf_op jit(solution)/shard_map/adjoint_window/pallas_call | solution.py:437
  40.7 2.1 %copy.8 = f32[1,6,256,128]{3,2,1,0:T(8,128)} copy(f32[1,6,256,128]{3,2,1,0:T(8,128)} %adjoint_window.1) | data formatting | bytes 1572864

commit v4 on v3

--- a/solution.py
+++ b/solution.py
@@ -25,7 +25,7 @@
 def body(
     forcing, courant_x, courant_y, faces_x, faces_y, coupling, out,
     nat_f, nat_o, even_odd, fr, op, cp, ops, ext_out, ext_in,
-    co, mix, r, x1, x2, r_n, x1_n, x2_n, adj, hand_out, hand_in, side_in, relay_in, res, outv,
+    co, mix, r, x1, x2, r_n, x1_n, x2_n, adj, hand_out, hand_in, side_out, side_in, relay_in, res, outv,
     load_sem, out_sem, part_send, part_recv, ext_send, ext_recv,
     hand_send, hand_recv, res_send, res_recv,
 ):
@@ -77,50 +77,47 @@
             device_id=partner, device_id_type=MESH,
         )
 
-    def ext_ends(slot, c, side):
-        n = EXT[slot][c]
-        if c == OPS:
-            start = (HALO + WIDTH - n, HALO)[side]
-            there = (HALO - n, HALO + WIDTH)[side]
-            return op.at[slot, :, :, pl.ds(start, n)], op.at[slot, :, :, pl.ds(there, n)]
-        return ext_out.at[side, c, :, pl.ds(0, 2 * n)], ext_in.at[slot, c, :, pl.ds(0, 2 * n)]
-
     def ext_pack(slot, c):
-        n = EXT[slot][c]
-        if c < OPS and n:
+        n, ref = EXT[slot][c], chunk(slot, c)
+        if n:
             for side in range(2):
                 start = (HALO + WIDTH - n, HALO)[side]
-                both = jnp.concatenate([fr[slot, c, :, p, start:start + n] for p in range(2)], axis=1)
-                ext_out[side, c, :, 0:2 * n] = both.astype(jnp.bfloat16)
+                both = jnp.concatenate([ref[:, p, start:start + n] for p in range(2)], axis=1)
+                ext_out[side, c, 0:both.shape[0], 0:2 * n] = both.astype(jnp.bfloat16)
 
     def ext_copies(slot, c):
-        if EXT[slot][c] == 0:
+        n, count = EXT[slot][c], chunk(slot, c).shape[0]
+        if n == 0:
             return []
-        copies = []
-        for side in range(2):
-            src, dst = ext_ends(slot, c, side)
-            copies.append(pltpu.make_async_remote_copy(
-                src_ref=src, dst_ref=dst,
+        return [
+            pltpu.make_async_remote_copy(
+                src_ref=ext_out.at[side, c, pl.ds(0, count), pl.ds(0, 2 * n)],
+                dst_ref=ext_in.at[slot, c, pl.ds(0, count), pl.ds(0, 2 * n)],
                 send_sem=ext_send.at[side, c], recv_sem=ext_recv.at[slot, c],
                 device_id=(to_east, to_west)[side], device_id_type=MESH,
-            ))
-        return copies
+            )
+            for side in range(2)
+        ]
+
+    def ext_start(slot, c):
+        for copy in ext_copies(slot, c):
+            copy.start()
+
+    def ext_sent(slot, c):
+        for copy in ext_copies(slot, c):
+            copy.wait_send()
 
     def ext_arrival(slot, c):
-        n = EXT[slot][c]
-        start = pl.multiple_of((HALO - n) * o + (HALO + WIDTH) * h, 8)
-        if c == OPS:
-            ref = op.at[slot, :, :, pl.ds(start, n)]
-        else:
-            ref = ext_in.at[slot, c, :, pl.ds(0, 2 * n)]
+        n, dest = EXT[slot][c], chunk(slot, c)
+        ref = ext_in.at[slot, c, pl.ds(0, dest.shape[0]), pl.ds(0, 2 * n)]
         pltpu.make_async_remote_copy(
             src_ref=ref, dst_ref=ref, send_sem=ext_send.at[0, c], recv_sem=ext_recv.at[slot, c],
             device_id=to_east, device_id_type=MESH,
         ).wait_recv()
-        if c < OPS:
-            both = ext_in[slot, c, :, 0:2 * n].astype(jnp.float32)
-            for p in range(2):
-                fr[slot, c, :, p, pl.ds(start, n)] = both[:, p * n:(p + 1) * n]
+        start = pl.multiple_of((HALO - n) * o + (HALO + WIDTH) * h, 8)
+        both = ext_in[slot, c, 0:dest.shape[0], 0:2 * n].astype(jnp.float32)
+        for p in range(2):
+            dest[:, p, pl.ds(start, n)] = both[:, p * n:(p + 1) * n]
 
     def wait_chunk(slot, c):
         @pl.when(h != slot)
@@ -152,16 +149,16 @@
             op[h, i, p, HALO:HALO + WIDTH] = jnp.transpose(nat_o[i, pl.ds(p, 128, stride=2), :])
     pl.semaphore_wait(barrier, count)
 
-    def send_first(c):
-        @pl.when(h == 1)
-        def _():
-            ext_pack(1, c)
-            for copy in ext_copies(1, c):
-                copy.start()
-
+    def send_chunk(c):
         partner_copy(c).start()
-
-    send_first(OPS)
+        for slot in range(2):
+            @pl.when(h == slot)
+            def _(slot=slot):
+                ext_pack(slot, c)
+                if slot == 1 and c >= 3:
+                    ext_start(slot, c)
+
+    send_chunk(OPS)
     for k in (3, 2, 1, 0):
         loads[5 + k].wait()
 
@@ -172,17 +169,22 @@
             return carry
 
         lax.fori_loop(0, F, one, 0)
-        send_first(k)
+        send_chunk(k)
         if k == 3:
             loads[4].wait()
             cp_copy(h).start()
 
-    @pl.when(h == 0)
-    def _():
-        for c in (OPS, 3, 2, 1, 0):
-            ext_pack(0, c)
-            for copy in ext_copies(0, c):
-                copy.start()
+    @pl.when(h == 1)
+    def _():
+        ext_sent(1, OPS)
+        ext_sent(1, 3)
+        ext_start(1, 2)
+
+    def second_halos():
+        @pl.when(h == 0)
+        def _():
+            for c in (OPS, 3, 2, 1, 0):
+                ext_start(0, c)
 
     lane = lax.broadcasted_iota(jnp.int32, (8, 128), 1)
 
@@ -281,6 +283,8 @@
                 @pl.when((k == c) & (pair == 1))
                 def _(c=c):
                     wait_chunk(slot, c)
+                    if slot == 1 and c == 2:
+                        second_halos()
 
             explicit(slot, k)
             return carry
@@ -317,29 +321,34 @@
             device_id=partner, device_id_type=MESH,
         )
 
-    def hand_main():
-        return pltpu.make_async_remote_copy(
-            src_ref=hand_out, dst_ref=hand_in, send_sem=hand_send.at[0], recv_sem=hand_recv.at[0],
+    def hand_main(f):
+        return pltpu.make_async_remote_copy(
+            src_ref=hand_out.at[f], dst_ref=hand_in.at[f], send_sem=hand_send.at[f], recv_sem=hand_recv.at[f],
             device_id=(h, space), device_id_type=MESH,
         )
 
     def hand_side():
         return pltpu.make_async_remote_copy(
-            src_ref=hand_out.at[:, :, pl.ds(pl.multiple_of(SIDE * h, SIDE), SIDE)], dst_ref=side_in,
-            send_sem=hand_send.at[1], recv_sem=hand_recv.at[1],
+            src_ref=side_out, dst_ref=side_in, send_sem=hand_send.at[F], recv_sem=hand_recv.at[F],
             device_id=(o, at_space(2 * h - 1)), device_id_type=MESH,
         )
 
-    def relay():
-        return pltpu.make_async_remote_copy(
-            src_ref=hand_in.at[:, :, pl.ds(pl.multiple_of(SIDE * o, SIDE), SIDE)], dst_ref=relay_in,
-            send_sem=hand_send.at[2], recv_sem=hand_recv.at[2],
+    def relay(f):
+        return pltpu.make_async_remote_copy(
+            src_ref=hand_in.at[f, :, pl.ds(pl.multiple_of(SIDE * o, SIDE), SIDE)], dst_ref=relay_in.at[f],
+            send_sem=hand_send.at[F + 1 + f], recv_sem=hand_recv.at[F + 1 + f],
             device_id=partner, device_id_type=MESH,
         )
 
     wait_chunk(1, OPS)
     coefficients(1)
 
+    @pl.when(h == 1)
+    def _():
+        ext_sent(1, 2)
+        ext_start(1, 1)
+        ext_start(1, 0)
+
     @pl.when(pair == 1)
     def _():
         wait_chunk(1, 3)
@@ -350,18 +359,25 @@
 
     @pl.when(pair == 0)
     def _():
+        second_halos()
+        for c in range(STEPS):
+            wait_chunk(1, c)
         wait_chunk(0, OPS)
         coefficients(0)
-        for slot in (1, 0):
-            for c in range(STEPS):
-                wait_chunk(slot, c)
-        hand_main().wait_recv()
-        relay().start()
-        adj[0, :, :, SIDE:SIDE + HALF] = hand_in[...].astype(jnp.float32)
+        for c in range(STEPS):
+            wait_chunk(0, c)
+        for f in range(F):
+            hand_main(f).wait_recv()
+            relay(f).start()
+            adj[0, f, :, SIDE:SIDE + HALF] = hand_in[f].astype(jnp.float32)
         hand_side().wait_recv()
-        adj[0, :, :, pl.ds(pl.multiple_of((SIDE + HALF) * h, SIDE), SIDE)] = side_in[...].astype(jnp.float32)
-        relay().wait_recv()
-        adj[0, :, :, pl.ds(pl.multiple_of((SIDE + HALF) * o, SIDE), SIDE)] = relay_in[...].astype(jnp.float32)
+        both = side_in[...].astype(jnp.float32)
+        for p in range(2):
+            start = pl.multiple_of((SIDE - HALO) * o + (SIDE + HALF) * h, 8)
+            adj[0, :, p, pl.ds(start, HALO)] = both[:, p * HALO:(p + 1) * HALO]
+        for f in range(F):
+            relay(f).wait_recv()
+            adj[0, f, :, pl.ds(pl.multiple_of((SIDE + HALF) * o, SIDE), SIDE)] = relay_in[f].astype(jnp.float32)
         from_adj(1)
 
     steps(1, pair)
@@ -383,9 +399,13 @@
 
     @pl.when(pair == 1)
     def _():
-        hand_out[...] = adj[1, :, :, SIDE:SIDE + HALF].astype(jnp.bfloat16)
+        start = pl.multiple_of(SIDE + (HALF - HALO) * h, 8)
+        both = jnp.concatenate([adj[1, :, p, pl.ds(start, HALO)] for p in range(2)], axis=1)
+        side_out[...] = both.astype(jnp.bfloat16)
         hand_side().start()
-        hand_main().start()
+        for f in range(F):
+            hand_out[f] = adj[1, f, :, SIDE:SIDE + HALF].astype(jnp.bfloat16)
+            hand_main(f).start()
 
     @pl.when(h == 1)
     def _():
@@ -405,12 +425,11 @@
 
     for c in range(STEPS + 1):
         partner_copy(c).wait_send()
-    for slot in range(2):
+    for slot, left in ((0, (OPS, 3, 2, 1)), (1, (1, 0))):
         @pl.when(h == slot)
-        def _(slot=slot):
-            for c in range(STEPS + 1):
-                for copy in ext_copies(slot, c):
-                    copy.wait_send()
+        def _(slot=slot, left=left):
+            for c in left:
+                ext_sent(slot, c)
 
     cp_copy(h).wait_send()
     for f in range(F):
@@ -418,12 +437,14 @@
 
     @pl.when(pair == 1)
     def _():
-        hand_main().wait_send()
         hand_side().wait_send()
+        for f in range(F):
+            hand_main(f).wait_send()
 
     @pl.when(pair == 0)
     def _():
-        relay().wait_send()
+        for f in range(F):
+            relay(f).wait_send()
 
     for f in range(F):
         out_copy(f).wait()
@@ -447,22 +468,23 @@
             pltpu.VMEM((2, 4, 2, ROWS, 128), f32),
             pltpu.VMEM((2, F, 1, F), f32),
             pltpu.VMEM((2, T + 2, 2, 8, 128), f32),
-            pltpu.VMEM((2, STEPS, F, 2 * HALO, 128), bf16),
-            pltpu.VMEM((2, STEPS, F, 2 * HALO, 128), bf16),
+            pltpu.VMEM((2, STEPS + 1, F, 2 * HALO, 128), bf16),
+            pltpu.VMEM((2, STEPS + 1, F, 2 * HALO, 128), bf16),
             pltpu.VMEM((2, T, 2, 9, 8, 128), f32),
             pltpu.VMEM((2, F, F, 8, 128), f32),
             state, state, state, beside, beside, beside,
             pltpu.VMEM((2, F, 2, HALF + 2 * SIDE, 128), f32),
             pltpu.VMEM((F, 2, HALF, 128), bf16),
             pltpu.VMEM((F, 2, HALF, 128), bf16),
-            pltpu.VMEM((F, 2, SIDE, 128), bf16),
+            pltpu.VMEM((F, 2 * HALO, 128), bf16),
+            pltpu.VMEM((F, 2 * HALO, 128), bf16),
             pltpu.VMEM((F, 2, SIDE, 128), bf16),
             pltpu.VMEM((F, 2, WIDTH, 128), f32),
             pltpu.VMEM((F, 256, 128), f32),
             dma((9,)), dma((F,)),
             dma((6,)), dma((6,)),
             dma((2, 5)), dma((2, 5)),
-            dma((3,)), dma((3,)),
+            dma((2 * F + 1,)), dma((2 * F + 1,)),
             dma((F,)), dma((F,)),
         ],
         compiler_params=pltpu.CompilerParams(

time: 43.2 us -> 46.7 us (1.081)
  Pallas kernels: 40.7 us -> 44.2 us
    pallas_call x1, Pallas kernels: 40.7 us -> 44.2 us  [per_device(): pl.pallas_call(body, out_shape=jax.ShapeDtypeStruct((1,) + forcing.shape[...]
where the time goes in v4:
time: 46.7 us; the launch traced here: 46.2 us
  Pallas kernels  44.2 us (95%)
  local copies, waits for them, and re-layouts  2.06 us (4%)
    pallas_call x1, Pallas kernels, per_device(): pl.pallas_call(body, out_shape=jax.ShapeDtypeStruct((1,) + forcing.shape[...  44.2 us
    unnamed x1, local copies, waits for them, and re-layouts  2.06 us

profile of v4, /device:TPU:0, one launch (start us, length us, event | category | flops | bytes accessed | tf_op | source)
XLA Modules:
  0.0 46.2 jit_solution(14690706071459925410)
XLA Ops:
  0.0 44.2 %adjoint_window.1 = f32[1,6,256,128]{3,2,1,0:T(8,128)} custom-call(bf16[1,4,6,256,128]{4,3,2,1,0:T(8,128)(2,1)} %forcing.1, f32[1,256,128]{2,1,0:T(8,128)} %courant_x.1, f32[1,256,128]{2,1,0:T(8,128)} %courant_y.1, f32[1,256,128]{2,1,0:T(8,128)} %faces_x.1, f32[1,256,128]{2,1,0:T(8,128)} %faces_y.1, f32[6,1,6]{2,1,0:T(1,128)} %bitcast.1), custom_call_target="tpu_custom_call" | custom-call | tf_op jit(solution)/shard_map/adjoint_window/pallas_call | solution.py:458
  44.2 2.1 %copy.8 = f32[1,6,256,128]{3,2,1,0:T(8,128)} copy(f32[1,6,256,128]{3,2,1,0:T(8,128)} %adjoint_window.1) | data formatting | bytes 1572864

commit v5 on v4

--- a/solution.py
+++ b/solution.py
@@ -147,18 +147,22 @@
     for i in range(4):
         for p in range(2):
             op[h, i, p, HALO:HALO + WIDTH] = jnp.transpose(nat_o[i, pl.ds(p, 128, stride=2), :])
-    pl.semaphore_wait(barrier, count)
-
     def send_chunk(c):
         partner_copy(c).start()
         for slot in range(2):
             @pl.when(h == slot)
             def _(slot=slot):
                 ext_pack(slot, c)
-                if slot == 1 and c >= 3:
+                if slot == 1:
                     ext_start(slot, c)
 
-    send_chunk(OPS)
+    early = lax.rem(space, 16) == 0
+
+    @pl.when(jnp.logical_not(early))
+    def _():
+        pl.semaphore_wait(barrier, count)
+        send_chunk(OPS)
+
     for k in (3, 2, 1, 0):
         loads[5 + k].wait()
 
@@ -169,22 +173,24 @@
             return carry
 
         lax.fori_loop(0, F, one, 0)
-        send_chunk(k)
-        if k == 3:
-            loads[4].wait()
-            cp_copy(h).start()
-
-    @pl.when(h == 1)
-    def _():
-        ext_sent(1, OPS)
-        ext_sent(1, 3)
-        ext_start(1, 2)
-
-    def second_halos():
-        @pl.when(h == 0)
-        def _():
-            for c in (OPS, 3, 2, 1, 0):
-                ext_start(0, c)
+
+        @pl.when(jnp.logical_not(early))
+        def _(k=k):
+            send_chunk(k)
+
+    @pl.when(early)
+    def _():
+        pl.semaphore_wait(barrier, count)
+        for c in (OPS, 3, 2, 1, 0):
+            send_chunk(c)
+
+    loads[4].wait()
+    cp_copy(h).start()
+
+    @pl.when(h == 0)
+    def _():
+        for c in (OPS, 3, 2, 1, 0):
+            ext_start(0, c)
 
     lane = lax.broadcasted_iota(jnp.int32, (8, 128), 1)
 
@@ -260,44 +266,53 @@
         lax.fori_loop(0, TS[slot], one, 0, unroll=UNROLL)
         pads(slot, dst)
 
-    def explicit(slot, k):
-        def one(t, carry):
-            for p in range(2):
-                value = fr[slot, k, :, p, frame(slot, t), :]
-                value = value + co[slot, t, p, 5] * x2[t + 2, p] + co[slot, t, p, 6] * x2[t, p]
-                value = value + co[slot, t, p, 7] * x2_n[t + 1, p] + co[slot, t, p, 8] * x2[t + 1, 1 - p]
-                for g in range(F):
-                    value = value + mix[slot, g] * x2[t + 1, p, g]
-                store(r, r_n, t, p, value)
-            return carry
-
-        lax.fori_loop(0, TS[slot], one, 0, unroll=UNROLL)
-        pads(slot, r)
+    def explicit_value(slot, k, t, p):
+        value = fr[slot, k, :, p, frame(slot, t), :]
+        value = value + co[slot, t, p, 5] * x2[t + 2, p] + co[slot, t, p, 6] * x2[t, p]
+        value = value + co[slot, t, p, 7] * x2_n[t + 1, p] + co[slot, t, p, 8] * x2[t + 1, 1 - p]
+        for g in range(F):
+            value = value + mix[slot, g] * x2[t + 1, p, g]
+        return value
+
+    def step(slot, n):
+        k = STEPS - 1 - n
+        sweep(slot, r, r_n, x1, x1_n, None)
+        sweep(slot, x1, x1_n, x2, x2_n, r)
+        for c in range(STEPS):
+            @pl.when((k == c) & (pair == 1))
+            def _(c=c):
+                wait_chunk(slot, c)
+
+        return k
 
     def steps(slot, first):
         def one(n, carry):
-            k = STEPS - 1 - n
-            sweep(slot, r, r_n, x1, x1_n, None)
-            sweep(slot, x1, x1_n, x2, x2_n, r)
-            for c in range(STEPS):
-                @pl.when((k == c) & (pair == 1))
-                def _(c=c):
-                    wait_chunk(slot, c)
-                    if slot == 1 and c == 2:
-                        second_halos()
-
-            explicit(slot, k)
+            k = step(slot, n)
+
+            def at(t, carry):
+                for p in range(2):
+                    store(r, r_n, t, p, explicit_value(slot, k, t, p))
+                return carry
+
+            lax.fori_loop(0, TS[slot], at, 0, unroll=UNROLL)
+            pads(slot, r)
             return carry
 
-        lax.fori_loop(first, STEPS, one, 0)
+        lax.fori_loop(first, STEPS - 1, one, 0)
+        step(slot, STEPS - 1)
+        for p in range(2):
+            def at(t, carry, p=p):
+                adj[1 - slot, :, p, adj_frame(slot, t), :] = explicit_value(slot, 0, t, p)
+                return carry
+
+            lax.fori_loop(0, TS[slot], at, 0, unroll=UNROLL)
+
+            @pl.when(h == 1 - slot)
+            def _(p=p):
+                result_copy(1 - slot, p).start()
 
     def adj_frame(slot, t):
         return pl.ds(SIDE - WEST[slot] + t, 8, stride=TS[slot])
-
-    def to_adj(slot):
-        for t in range(TS[slot]):
-            for p in range(2):
-                adj[1 - slot, :, p, adj_frame(slot, t), :] = r[t + 1, p]
 
     def from_adj(slot):
         for t in range(TS[slot]):
@@ -305,49 +320,48 @@
                 store(r, r_n, t, p, adj[0, :, p, adj_frame(slot, t), :])
         pads(slot, r)
 
-    def result_copy(phase, f):
-        return pltpu.make_async_remote_copy(
-            src_ref=adj.at[phase, f, :, pl.ds(SIDE, HALF)],
-            dst_ref=res.at[f, :, pl.ds(pl.multiple_of(HALF * h, HALF), HALF)],
-            send_sem=res_send.at[f], recv_sem=res_recv.at[f],
+    def result_copy(phase, p):
+        return pltpu.make_async_remote_copy(
+            src_ref=adj.at[phase, :, p, pl.ds(SIDE, HALF)],
+            dst_ref=res.at[:, p, pl.ds(pl.multiple_of(HALF * h, HALF), HALF)],
+            send_sem=res_send.at[p], recv_sem=res_recv.at[p],
             device_id=partner, device_id_type=MESH,
         )
 
-    def result_arrival(f):
-        return pltpu.make_async_remote_copy(
-            src_ref=adj.at[0, f, :, pl.ds(SIDE, HALF)],
-            dst_ref=res.at[f, :, pl.ds(pl.multiple_of(HALF * o, HALF), HALF)],
-            send_sem=res_send.at[f], recv_sem=res_recv.at[f],
+    def result_arrival(p):
+        return pltpu.make_async_remote_copy(
+            src_ref=adj.at[0, :, p, pl.ds(SIDE, HALF)],
+            dst_ref=res.at[:, p, pl.ds(pl.multiple_of(HALF * o, HALF), HALF)],
+            send_sem=res_send.at[p], recv_sem=res_recv.at[p],
             device_id=partner, device_id_type=MESH,
         )
 
-    def hand_main(f):
-        return pltpu.make_async_remote_copy(
-            src_ref=hand_out.at[f], dst_ref=hand_in.at[f], send_sem=hand_send.at[f], recv_sem=hand_recv.at[f],
+    PIECES = [(inner, g) for inner in (True, False) for g in range(2)]
+
+    def hand_main(n):
+        inner, g = PIECES[n]
+        ref = (pl.ds(F // 2 * g, F // 2), slice(None), pl.ds(pl.multiple_of(SIDE * (o if inner else h), SIDE), SIDE))
+        return pltpu.make_async_remote_copy(
+            src_ref=hand_out.at[ref], dst_ref=hand_in.at[ref], send_sem=hand_send.at[n], recv_sem=hand_recv.at[n],
             device_id=(h, space), device_id_type=MESH,
         )
 
     def hand_side():
         return pltpu.make_async_remote_copy(
-            src_ref=side_out, dst_ref=side_in, send_sem=hand_send.at[F], recv_sem=hand_recv.at[F],
+            src_ref=side_out, dst_ref=side_in, send_sem=hand_send.at[4], recv_sem=hand_recv.at[4],
             device_id=(o, at_space(2 * h - 1)), device_id_type=MESH,
         )
 
-    def relay(f):
-        return pltpu.make_async_remote_copy(
-            src_ref=hand_in.at[f, :, pl.ds(pl.multiple_of(SIDE * o, SIDE), SIDE)], dst_ref=relay_in.at[f],
-            send_sem=hand_send.at[F + 1 + f], recv_sem=hand_recv.at[F + 1 + f],
+    def relay(g):
+        fields = pl.ds(F // 2 * g, F // 2)
+        return pltpu.make_async_remote_copy(
+            src_ref=hand_in.at[fields, :, pl.ds(pl.multiple_of(SIDE * o, SIDE), SIDE)], dst_ref=relay_in.at[fields],
+            send_sem=hand_send.at[5 + g], recv_sem=hand_recv.at[5 + g],
             device_id=partner, device_id_type=MESH,
         )
 
     wait_chunk(1, OPS)
     coefficients(1)
-
-    @pl.when(h == 1)
-    def _():
-        ext_sent(1, 2)
-        ext_start(1, 1)
-        ext_start(1, 0)
 
     @pl.when(pair == 1)
     def _():
@@ -359,34 +373,34 @@
 
     @pl.when(pair == 0)
     def _():
-        second_halos()
         for c in range(STEPS):
             wait_chunk(1, c)
         wait_chunk(0, OPS)
         coefficients(0)
         for c in range(STEPS):
             wait_chunk(0, c)
-        for f in range(F):
-            hand_main(f).wait_recv()
-            relay(f).start()
-            adj[0, f, :, SIDE:SIDE + HALF] = hand_in[f].astype(jnp.float32)
+        def take(fields, inner):
+            rows = pl.multiple_of(SIDE * (o if inner else h), SIDE)
+            adj[0, fields, :, pl.ds(SIDE + rows, SIDE)] = hand_in[fields, :, pl.ds(rows, SIDE)].astype(jnp.float32)
+
+        for g in range(2):
+            hand_main(g).wait_recv()
+            relay(g).start()
+            take(slice(F // 2 * g, F // 2 * (g + 1)), True)
         hand_side().wait_recv()
         both = side_in[...].astype(jnp.float32)
         for p in range(2):
             start = pl.multiple_of((SIDE - HALO) * o + (SIDE + HALF) * h, 8)
             adj[0, :, p, pl.ds(start, HALO)] = both[:, p * HALO:(p + 1) * HALO]
-        for f in range(F):
-            relay(f).wait_recv()
-            adj[0, f, :, pl.ds(pl.multiple_of((SIDE + HALF) * o, SIDE), SIDE)] = relay_in[f].astype(jnp.float32)
+        for g in range(2):
+            relay(g).wait_recv()
+        adj[0, :, :, pl.ds(pl.multiple_of((SIDE + HALF) * o, SIDE), SIDE)] = relay_in[...].astype(jnp.float32)
+        for g in range(2):
+            hand_main(2 + g).wait_recv()
+            take(slice(F // 2 * g, F // 2 * (g + 1)), False)
         from_adj(1)
 
     steps(1, pair)
-    to_adj(1)
-
-    @pl.when(h == 0)
-    def _():
-        for f in range(F):
-            result_copy(0, f).start()
 
     @pl.when(pair == 1)
     def _():
@@ -395,7 +409,6 @@
 
     from_adj(0)
     steps(0, 0)
-    to_adj(0)
 
     @pl.when(pair == 1)
     def _():
@@ -403,48 +416,48 @@
         both = jnp.concatenate([adj[1, :, p, pl.ds(start, HALO)] for p in range(2)], axis=1)
         side_out[...] = both.astype(jnp.bfloat16)
         hand_side().start()
-        for f in range(F):
-            hand_out[f] = adj[1, f, :, SIDE:SIDE + HALF].astype(jnp.bfloat16)
-            hand_main(f).start()
-
-    @pl.when(h == 1)
-    def _():
-        for f in range(F):
-            result_copy(1, f).start()
+        for g in range(2):
+            fields = slice(F // 2 * g, F // 2 * (g + 1))
+            hand_out[fields] = adj[1, fields, :, SIDE:SIDE + HALF].astype(jnp.bfloat16)
+            hand_main(g).start()
+        for g in range(2):
+            hand_main(2 + g).start()
 
     def out_copy(f):
         return pltpu.make_async_copy(outv.at[f], out.at[0, f], out_sem.at[f])
 
     own = adj.at[1 - h]
     res[:, :, pl.ds(pl.multiple_of(HALF * h, HALF), HALF)] = own[:, :, SIDE:SIDE + HALF]
+    result_arrival(0).wait_recv()
     for f in range(F):
-        result_arrival(f).wait_recv()
-        for p in range(2):
-            outv[f, pl.ds(p, 128, stride=2), :] = jnp.transpose(res[f, p])
+        outv[f, pl.ds(0, 128, stride=2), :] = jnp.transpose(res[f, 0])
+    result_arrival(1).wait_recv()
+    for f in range(F):
+        outv[f, pl.ds(1, 128, stride=2), :] = jnp.transpose(res[f, 1])
         out_copy(f).start()
 
     for c in range(STEPS + 1):
         partner_copy(c).wait_send()
-    for slot, left in ((0, (OPS, 3, 2, 1)), (1, (1, 0))):
+    for slot, left in ((0, (OPS, 3, 2, 1)), (1, (OPS, 3, 2, 1, 0))):
         @pl.when(h == slot)
         def _(slot=slot, left=left):
             for c in left:
                 ext_sent(slot, c)
 
     cp_copy(h).wait_send()
-    for f in range(F):
-        result_copy(0, f).wait_send()
+    for p in range(2):
+        result_copy(0, p).wait_send()
 
     @pl.when(pair == 1)
     def _():
         hand_side().wait_send()
-        for f in range(F):
-            hand_main(f).wait_send()
+        for n in range(4):
+            hand_main(n).wait_send()
 
     @pl.when(pair == 0)
     def _():
-        for f in range(F):
-            relay(f).wait_send()
+        for g in range(2):
+            relay(g).wait_send()
 
     for f in range(F):
         out_copy(f).wait()
@@ -484,8 +497,8 @@
             dma((9,)), dma((F,)),
             dma((6,)), dma((6,)),
             dma((2, 5)), dma((2, 5)),
-            dma((2 * F + 1,)), dma((2 * F + 1,)),
-            dma((F,)), dma((F,)),
+            dma((7,)), dma((7,)),
+            dma((2,)), dma((2,)),
         ],
         compiler_params=pltpu.CompilerParams(
             collective_id=0, has_side_effects=True, vmem_limit_bytes=60 * 1024 * 1024

time: 46.7 us -> 42.3 us (0.906)
  Pallas kernels: 44.2 us -> 40.1 us
    pallas_call x1, Pallas kernels: 44.2 us -> 40.1 us  [per_device(): pl.pallas_call(body, out_shape=jax.ShapeDtypeStruct((1,) + forcing.shape[...]
where the time goes in v5:
time: 42.3 us; the launch traced here: 42.2 us
  Pallas kernels  40.1 us (95%)
  local copies, waits for them, and re-layouts  2.06 us (5%)
    pallas_call x1, Pallas kernels, per_device(): pl.pallas_call(body, out_shape=jax.ShapeDtypeStruct((1,) + forcing.shape[...  40.1 us
    unnamed x1, local copies, waits for them, and re-layouts  2.06 us

profile of v5, /device:TPU:0, one launch (start us, length us, event | category | flops | bytes accessed | tf_op | source)
XLA Modules:
  0.0 42.2 jit_solution(2469626463291930232)
XLA Ops:
  0.0 40.1 %adjoint_window.1 = f32[1,6,256,128]{3,2,1,0:T(8,128)} custom-call(bf16[1,4,6,256,128]{4,3,2,1,0:T(8,128)(2,1)} %forcing.1, f32[1,256,128]{2,1,0:T(8,128)} %courant_x.1, f32[1,256,128]{2,1,0:T(8,128)} %courant_y.1, f32[1,256,128]{2,1,0:T(8,128)} %faces_x.1, f32[1,256,128]{2,1,0:T(8,128)} %faces_y.1, f32[6,1,6]{2,1,0:T(1,128)} %bitcast.1), custom_call_target="tpu_custom_call" | custom-call | tf_op jit(solution)/shard_map/adjoint_window/pallas_call | solution.py:471
  40.1 2.1 %copy.8 = f32[1,6,256,128]{3,2,1,0:T(8,128)} copy(f32[1,6,256,128]{3,2,1,0:T(8,128)} %adjoint_window.1) | data formatting | bytes 1572864

commit v6 on v5

--- a/solution.py
+++ b/solution.py
@@ -25,7 +25,7 @@
 def body(
     forcing, courant_x, courant_y, faces_x, faces_y, coupling, out,
     nat_f, nat_o, even_odd, fr, op, cp, ops, ext_out, ext_in,
-    co, mix, r, x1, x2, r_n, x1_n, x2_n, adj, hand_out, hand_in, side_out, side_in, relay_in, res, outv,
+    co, mix, r, x1, x2, flux, r_n, x1_n, x2_n, adj, hand_out, hand_in, side_out, side_in, relay_in, res, outv,
     load_sem, out_sem, part_send, part_recv, ext_send, ext_recv,
     hand_send, hand_recv, res_send, res_recv,
 ):
@@ -209,12 +209,10 @@
                 value = jnp.broadcast_to(row[:, f:f + 1], (8, 128))
                 mix[slot, g, f] = OMEGA * (value + 1.0) if g == f else OMEGA * value
 
-        for i in (0, 2):
-            for p in range(2):
-                for t in range(last):
-                    ops[i // 2, t + 1, p] = op[slot, i, p, frame(slot, t), :]
-                ops[i // 2, 0, p] = pltpu.roll(ops[i // 2, last, p], 1, 0)
-                ops[i // 2, last + 1, p] = pltpu.roll(ops[i // 2, 1, p], 7, 0)
+        for p in range(2):
+            for t in range(last):
+                ops[t + 1, p] = op[slot, 0, p, frame(slot, t), :]
+            ops[0, p] = pltpu.roll(ops[last, p], 1, 0)
 
         def one(t, carry):
             def get(i, p):
@@ -227,16 +225,15 @@
             v_north = (v1, jnp.where(lane == 127, 0.0, pltpu.roll(v0, 127, 1)))
             v_south = (jnp.where(lane == 0, 0.0, -pltpu.roll(v1, 1, 1)), -v0)
             for p in range(2):
-                east, west = OMEGA * ops[0, t + 1, p], OMEGA * ops[0, t, p]
+                east, west = OMEGA * ops[t + 1, p], OMEGA * ops[t, p]
                 co[slot, t, p, 0] = (1.0 - OMEGA) - (east + west + north[p] + south[p])
                 co[slot, t, p, 1] = east
                 co[slot, t, p, 2] = west
                 co[slot, t, p, 3] = (south, north)[p][p]
                 co[slot, t, p, 4] = (north, south)[p][p]
-                co[slot, t, p, 5] = 0.5 * OMEGA * ops[1, t + 2, p]
-                co[slot, t, p, 6] = -0.5 * OMEGA * ops[1, t, p]
-                co[slot, t, p, 7] = (v_south, v_north)[p][p]
-                co[slot, t, p, 8] = (v_north, v_south)[p][p]
+                co[slot, t, p, 5] = 0.5 * OMEGA * get(2, p)
+                co[slot, t, p, 6] = (v_south, v_north)[p][p]
+                co[slot, t, p, 7] = (v_north, v_south)[p][p]
             return carry
 
         lax.fori_loop(0, last, one, 0)
@@ -261,15 +258,17 @@
                 value = value + co[slot, t, p, 1] * src[t + 2, p] + co[slot, t, p, 2] * src[t, p]
                 value = value + co[slot, t, p, 3] * src_n[t + 1, p] + co[slot, t, p, 4] * src[t + 1, 1 - p]
                 store(dst, dst_n, t, p, value)
+                if add is not None:
+                    flux[t + 1, p] = co[slot, t, p, 5] * value
             return carry
 
         lax.fori_loop(0, TS[slot], one, 0, unroll=UNROLL)
-        pads(slot, dst)
+        pads(slot, dst if add is None else flux)
 
     def explicit_value(slot, k, t, p):
         value = fr[slot, k, :, p, frame(slot, t), :]
-        value = value + co[slot, t, p, 5] * x2[t + 2, p] + co[slot, t, p, 6] * x2[t, p]
-        value = value + co[slot, t, p, 7] * x2_n[t + 1, p] + co[slot, t, p, 8] * x2[t + 1, 1 - p]
+        value = value + flux[t + 2, p] - flux[t, p]
+        value = value + co[slot, t, p, 6] * x2_n[t + 1, p] + co[slot, t, p, 7] * x2[t + 1, 1 - p]
         for g in range(F):
             value = value + mix[slot, g] * x2[t + 1, p, g]
         return value
@@ -480,12 +479,12 @@
             pltpu.VMEM((2, STEPS, F, 2, ROWS, 128), f32),
             pltpu.VMEM((2, 4, 2, ROWS, 128), f32),
             pltpu.VMEM((2, F, 1, F), f32),
-            pltpu.VMEM((2, T + 2, 2, 8, 128), f32),
+            pltpu.VMEM((T + 1, 2, 8, 128), f32),
             pltpu.VMEM((2, STEPS + 1, F, 2 * HALO, 128), bf16),
             pltpu.VMEM((2, STEPS + 1, F, 2 * HALO, 128), bf16),
-            pltpu.VMEM((2, T, 2, 9, 8, 128), f32),
+            pltpu.VMEM((2, T, 2, 8, 8, 128), f32),
             pltpu.VMEM((2, F, F, 8, 128), f32),
-            state, state, state, beside, beside, beside,
+            state, state, state, state, beside, beside, beside,
             pltpu.VMEM((2, F, 2, HALF + 2 * SIDE, 128), f32),
             pltpu.VMEM((F, 2, HALF, 128), bf16),
             pltpu.VMEM((F, 2, HALF, 128), bf16),

time: 42.3 us -> 41.8 us (0.988)
  Pallas kernels: 40.1 us -> 39.5 us
    pallas_call x1, Pallas kernels: 40.1 us -> 39.5 us  [per_device(): pl.pallas_call(body, out_shape=jax.ShapeDtypeStruct((1,) + forcing.shape[...]
where the time goes in v6:
time: 41.8 us; the launch traced here: 41.6 us
  Pallas kernels  39.5 us (94%)
  local copies, waits for them, and re-layouts  2.06 us (5%)
    pallas_call x1, Pallas kernels, per_device(): pl.pallas_call(body, out_shape=jax.ShapeDtypeStruct((1,) + forcing.shape[...  39.5 us
    unnamed x1, local copies, waits for them, and re-layouts  2.06 us

profile of v6, /device:TPU:0, one launch (start us, length us, event | category | flops | bytes accessed | tf_op | source)
XLA Modules:
  0.0 41.6 jit_solution(8454717794306977427)
XLA Ops:
  0.0 39.5 %adjoint_window.1 = f32[1,6,256,128]{3,2,1,0:T(8,128)} custom-call(bf16[1,4,6,256,128]{4,3,2,1,0:T(8,128)(2,1)} %forcing.1, f32[1,256,128]{2,1,0:T(8,128)} %courant_x.1, f32[1,256,128]{2,1,0:T(8,128)} %courant_y.1, f32[1,256,128]{2,1,0:T(8,128)} %faces_x.1, f32[1,256,128]{2,1,0:T(8,128)} %faces_y.1, f32[6,1,6]{2,1,0:T(1,128)} %bitcast.1), custom_call_target="tpu_custom_call" | custom-call | tf_op jit(solution)/shard_map/adjoint_window/pallas_call | solution.py:470
  39.6 2.1 %copy.8 = f32[1,6,256,128]{3,2,1,0:T(8,128)} copy(f32[1,6,256,128]{3,2,1,0:T(8,128)} %adjoint_window.1) | data formatting | bytes 1572864

commit v7 on v6

--- a/solution.py
+++ b/solution.py
@@ -53,7 +53,7 @@
     loads = [pltpu.make_async_copy(ops_in[i].at[0], nat_o.at[i], load_sem.at[i]) for i in range(4)]
     loads.append(pltpu.make_async_copy(coupling, cp.at[h], load_sem.at[4]))
     loads += [pltpu.make_async_copy(forcing.at[0, k], nat_f.at[k], load_sem.at[5 + k]) for k in range(STEPS)]
-    for i in (0, 1, 2, 3, 8, 4, 7, 6, 5):
+    for i in (0, 1, 2, 3, 8):
         loads[i].start()
 
     partner = (2 * pair + o, space)
@@ -144,6 +144,8 @@
 
     for i in range(4):
         loads[i].wait()
+    for i in (4, 7, 6, 5):
+        loads[i].start()
     for i in range(4):
         for p in range(2):
             op[h, i, p, HALO:HALO + WIDTH] = jnp.transpose(nat_o[i, pl.ds(p, 128, stride=2), :])
@@ -308,7 +310,8 @@
 
             @pl.when(h == 1 - slot)
             def _(p=p):
-                result_copy(1 - slot, p).start()
+                for n in ((0,), (1, 2))[p]:
+                    result_copy(1 - slot, n).start()
 
     def adj_frame(slot, t):
         return pl.ds(SIDE - WEST[slot] + t, 8, stride=TS[slot])
@@ -319,19 +322,25 @@
                 store(r, r_n, t, p, adj[0, :, p, adj_frame(slot, t), :])
         pads(slot, r)
 
-    def result_copy(phase, p):
-        return pltpu.make_async_remote_copy(
-            src_ref=adj.at[phase, :, p, pl.ds(SIDE, HALF)],
-            dst_ref=res.at[:, p, pl.ds(pl.multiple_of(HALF * h, HALF), HALF)],
-            send_sem=res_send.at[p], recv_sem=res_recv.at[p],
+    PARTS = [(0, slice(0, F)), (1, slice(0, F // 2)), (1, slice(F // 2, F))]
+
+    def result_copy(phase, n):
+        p, fields = PARTS[n]
+        fields = pl.ds(fields.start, fields.stop - fields.start)
+        return pltpu.make_async_remote_copy(
+            src_ref=adj.at[phase, fields, p, pl.ds(SIDE, HALF)],
+            dst_ref=res.at[fields, p, pl.ds(pl.multiple_of(HALF * h, HALF), HALF)],
+            send_sem=res_send.at[n], recv_sem=res_recv.at[n],
             device_id=partner, device_id_type=MESH,
         )
 
-    def result_arrival(p):
-        return pltpu.make_async_remote_copy(
-            src_ref=adj.at[0, :, p, pl.ds(SIDE, HALF)],
-            dst_ref=res.at[:, p, pl.ds(pl.multiple_of(HALF * o, HALF), HALF)],
-            send_sem=res_send.at[p], recv_sem=res_recv.at[p],
+    def result_arrival(n):
+        p, fields = PARTS[n]
+        fields = pl.ds(fields.start, fields.stop - fields.start)
+        return pltpu.make_async_remote_copy(
+            src_ref=adj.at[0, fields, p, pl.ds(SIDE, HALF)],
+            dst_ref=res.at[fields, p, pl.ds(pl.multiple_of(HALF * o, HALF), HALF)],
+            send_sem=res_send.at[n], recv_sem=res_recv.at[n],
             device_id=partner, device_id_type=MESH,
         )
 
@@ -427,13 +436,13 @@
 
     own = adj.at[1 - h]
     res[:, :, pl.ds(pl.multiple_of(HALF * h, HALF), HALF)] = own[:, :, SIDE:SIDE + HALF]
-    result_arrival(0).wait_recv()
-    for f in range(F):
-        outv[f, pl.ds(0, 128, stride=2), :] = jnp.transpose(res[f, 0])
-    result_arrival(1).wait_recv()
-    for f in range(F):
-        outv[f, pl.ds(1, 128, stride=2), :] = jnp.transpose(res[f, 1])
-        out_copy(f).start()
+    for n in range(3):
+        result_arrival(n).wait_recv()
+        p, fields = PARTS[n]
+        for f in range(fields.start, fields.stop):
+            outv[f, pl.ds(p, 128, stride=2), :] = jnp.transpose(res[f, p])
+            if p == 1:
+                out_copy(f).start()
 
     for c in range(STEPS + 1):
         partner_copy(c).wait_send()
@@ -444,8 +453,8 @@
                 ext_sent(slot, c)
 
     cp_copy(h).wait_send()
-    for p in range(2):
-        result_copy(0, p).wait_send()
+    for n in range(3):
+        result_copy(0, n).wait_send()
 
     @pl.when(pair == 1)
     def _():
@@ -497,7 +506,7 @@
             dma((6,)), dma((6,)),
             dma((2, 5)), dma((2, 5)),
             dma((7,)), dma((7,)),
-            dma((2,)), dma((2,)),
+            dma((3,)), dma((3,)),
         ],
         compiler_params=pltpu.CompilerParams(
             collective_id=0, has_side_effects=True, vmem_limit_bytes=60 * 1024 * 1024

time: 41.8 us -> 41.9 us (level)
  no operation moved by 1% of the time
where the time goes in v7:
time: 41.9 us; the launch traced here: 41.7 us
  Pallas kernels  39.6 us (95%)
  local copies, waits for them, and re-layouts  2.06 us (5%)
    pallas_call x1, Pallas kernels, per_device(): pl.pallas_call(body, out_shape=jax.ShapeDtypeStruct((1,) + forcing.shape[...  39.6 us
    unnamed x1, local copies, waits for them, and re-layouts  2.06 us

profile of v7, /device:TPU:0, one launch (start us, length us, event | category | flops | bytes accessed | tf_op | source)
XLA Modules:
  0.0 41.7 jit_solution(6628905503294008809)
XLA Ops:
  0.0 39.6 %adjoint_window.1 = f32[1,6,256,128]{3,2,1,0:T(8,128)} custom-call(bf16[1,4,6,256,128]{4,3,2,1,0:T(8,128)(2,1)} %forcing.1, f32[1,256,128]{2,1,0:T(8,128)} %courant_x.1, f32[1,256,128]{2,1,0:T(8,128)} %courant_y.1, f32[1,256,128]{2,1,0:T(8,128)} %faces_x.1, f32[1,256,128]{2,1,0:T(8,128)} %faces_y.1, f32[6,1,6]{2,1,0:T(1,128)} %bitcast.1), custom_call_target="tpu_custom_call" | custom-call | tf_op jit(solution)/shard_map/adjoint_window/pallas_call | solution.py:479
  39.6 2.1 %copy.8 = f32[1,6,256,128]{3,2,1,0:T(8,128)} copy(f32[1,6,256,128]{3,2,1,0:T(8,128)} %adjoint_window.1) | data formatting | bytes 1572864

commit v8 on v6

--- a/solution.py
+++ b/solution.py
@@ -39,6 +39,13 @@
     def at_space(d):
         return lax.rem(space + d + n_space, n_space)
 
+    ops_in = (faces_x, faces_y, courant_x, courant_y)
+    loads = [pltpu.make_async_copy(ops_in[i].at[0], nat_o.at[i], load_sem.at[i]) for i in range(4)]
+    loads.append(pltpu.make_async_copy(coupling, cp.at[h], load_sem.at[4]))
+    loads += [pltpu.make_async_copy(forcing.at[0, k], nat_f.at[k], load_sem.at[5 + k]) for k in range(STEPS)]
+    for i in (0, 1, 2, 3, 8):
+        loads[i].start()
+
     barrier = pltpu.get_barrier_semaphore()
     count = 0
     for d in (-1, 1, 0):
@@ -48,13 +55,6 @@
             other = lax.rem(tm + j, 4)
             pl.semaphore_signal(barrier, inc=1, device_id=(other, at_space(d)), device_id_type=MESH)
             count += 1
-
-    ops_in = (faces_x, faces_y, courant_x, courant_y)
-    loads = [pltpu.make_async_copy(ops_in[i].at[0], nat_o.at[i], load_sem.at[i]) for i in range(4)]
-    loads.append(pltpu.make_async_copy(coupling, cp.at[h], load_sem.at[4]))
-    loads += [pltpu.make_async_copy(forcing.at[0, k], nat_f.at[k], load_sem.at[5 + k]) for k in range(STEPS)]
-    for i in (0, 1, 2, 3, 8, 4, 7, 6, 5):
-        loads[i].start()
 
     partner = (2 * pair + o, space)
     to_east = (2 * pair, at_space(1))
@@ -144,6 +144,8 @@
 
     for i in range(4):
         loads[i].wait()
+    for i in (4, 7, 6, 5):
+        loads[i].start()
     for i in range(4):
         for p in range(2):
             op[h, i, p, HALO:HALO + WIDTH] = jnp.transpose(nat_o[i, pl.ds(p, 128, stride=2), :])

time: 41.8 us -> 41.8 us (level)
  no operation moved by 1% of the time
where the time goes in v8:
time: 41.8 us; the launch traced here: 41.6 us
  Pallas kernels  39.5 us (94%)
  local copies, waits for them, and re-layouts  2.06 us (5%)
    pallas_call x1, Pallas kernels, per_device(): pl.pallas_call(body, out_shape=jax.ShapeDtypeStruct((1,) + forcing.shape[...  39.5 us
    unnamed x1, local copies, waits for them, and re-layouts  2.06 us

profile of v8, /device:TPU:0, one launch (start us, length us, event | category | flops | bytes accessed | tf_op | source)
XLA Modules:
  0.0 41.6 jit_solution(5914230559587704595)
XLA Ops:
  0.0 39.5 %adjoint_window.1 = f32[1,6,256,128]{3,2,1,0:T(8,128)} custom-call(bf16[1,4,6,256,128]{4,3,2,1,0:T(8,128)(2,1)} %forcing.1, f32[1,256,128]{2,1,0:T(8,128)} %courant_x.1, f32[1,256,128]{2,1,0:T(8,128)} %courant_y.1, f32[1,256,128]{2,1,0:T(8,128)} %faces_x.1, f32[1,256,128]{2,1,0:T(8,128)} %faces_y.1, f32[6,1,6]{2,1,0:T(1,128)} %bitcast.1), custom_call_target="tpu_custom_call" | custom-call | tf_op jit(solution)/shard_map/adjoint_window/pallas_call | solution.py:472
  39.6 2.1 %copy.8 = f32[1,6,256,128]{3,2,1,0:T(8,128)} copy(f32[1,6,256,128]{3,2,1,0:T(8,128)} %adjoint_window.1) | data formatting | bytes 1572864
